TPU v7x, 32 devices: a whole 2x2x4 slice. The times are simulated.
32 devices in a mesh: batch: 4 (over y, core), rows: 8 (over z, x).
Axes of the slice: x: 2, y: 2, z: 4, core: 2. Of those that a mesh axis runs over, the one named last changes fastest.
Arguments:
- features: float32 [4, 16384, 100], P('batch', 'rows'), may hold values from -6 to 6
- edge_rows: int32 [4, 8, 2, 16384], P('batch', 'rows'), may hold values from 0 to 3071, as said below
- edge_weight: float32 [4, 8, 16384], P('batch', 'rows'), may hold values from 0.02 to 0.2
- halo_counts: int32 [4, 8, 2], P('batch', 'rows'), may hold values from 1 to 512
- labels: int32 [4, 16384], P('batch', 'rows'), may hold values from 0 to 46
- pair_rows: int32 [4, 8, 8, 4], P('batch', 'rows'), may hold values from 0 to 2047
- step: int32 [1], replicated, may hold values from 2 to 20
- w_in: float32 [100, 256], P(None, 'batch'), may hold values from -0.625 to 0.625
- w_conv: float32 [3, 512, 256], P(None, 'batch'), may hold values from -0.25 to 0.25
- w_head: float32 [256, 47], P('batch'), may hold values from -0.375 to 0.375
- biases: float32 [4, 256], replicated, may hold values from -1 to 1
- norm_params: float32 [3, 2, 256], replicated, may hold values from 0.5 to 1.5
- head_bias: float32 [47], replicated, may hold values from -2 to 2
- mom_in: float32 [100, 256], P(None, 'batch'), may hold values from -0.0234375 to 0.0234375
- mom_conv: float32 [3, 512, 256], P(None, 'batch'), may hold values from -0.0234375 to 0.0234375
- mom_head: float32 [256, 47], P('batch'), may hold values from -0.0234375 to 0.0234375
- first_bias: float32 [4, 256], replicated, may hold values from -0.0024414062 to 0.0024414062
- first_norm: float32 [3, 2, 256], replicated, may hold values from -0.0024414062 to 0.0024414062
- first_head: float32 [47], replicated, may hold values from -0.0024414062 to 0.0024414062
- second_bias: float32 [4, 256], replicated, as said below
- second_norm: float32 [3, 2, 256], replicated, as said below
- second_head: float32 [47], replicated, as said below
Outputs:
- loss: float32 [], replicated
- new_w_in: float32 [100, 256], P(None, 'batch')
- new_w_conv: float32 [3, 512, 256], P(None, 'batch')
- new_w_head: float32 [256, 47], P('batch')
- new_mom_in: float32 [100, 256], P(None, 'batch')
- new_mom_conv: float32 [3, 512, 256], P(None, 'batch')
- new_mom_head: float32 [256, 47], P('batch')
- new_biases: float32 [4, 256], replicated
- new_norm_params: float32 [3, 2, 256], replicated
- new_head_bias: float32 [47], replicated
- new_first_bias: float32 [4, 256], replicated
- new_first_norm: float32 [3, 2, 256], replicated
- new_first_head: float32 [47], replicated
- new_second_bias: float32 [4, 256], replicated
- new_second_norm: float32 [3, 2, 256], replicated
- new_second_head: float32 [47], replicated
Inputs may be any that keep to these rules, and one draw needn't show every extreme that they name: edge_rows[b,r,0] are rows of block r; edge_rows[b,r,1] index the extended block and lie between 512 - halo_counts[b,r,0] and 2560 + halo_counts[b,r,1] - 1. `second_bias`: positive. `second_norm`: positive. `second_head`: positive.
All inputs are finite; a program needn't handle non-finite values.
Results may differ from a plain program's by a relative error of at most 0.002.
Values sent between devices are 32-bit elements; how exact they have to be, the bound alone decides.
A program may use at most 128 MiB of HBM per device.

v0:
```python
import math

import jax
import jax.numpy as jnp
from jax import lax
from jax.sharding import PartitionSpec as P

NS_STEPS = 5


highest = lax.Precision.HIGHEST
norm_epsilon = 1e-05
pair_weight = 0.05
newton_a = 3.4445
newton_b = -4.775
newton_c = 2.0315
muon_decay = 0.9
muon_rate = 0.5
muon_shrink = 0.01
adam_first_decay = 0.9
adam_second_decay = 0.999
adam_epsilon = 1e-08
adam_rate = 0.1
adam_shrink = 0.01


def extended(cells, sides, width):
    for axis, dim in sides:
        count = lax.axis_size(axis)
        ends = count - 1
        head = lax.slice_in_dim(cells, 0, width, axis=dim)
        tail = lax.slice_in_dim(cells, cells.shape[dim] - width, cells.shape[dim], axis=dim)
        cells = jnp.concatenate(
            [
                lax.ppermute(tail, axis, [(i, (i + 1) % count) for i in range(ends)]),
                cells,
                lax.ppermute(head, axis, [((i + 1) % count, i) for i in range(ends)]),
            ],
            axis=dim,
        )
    return cells


def passed_along(array, axis, by):
    count = lax.axis_size(axis)
    pairs = [(i, i + by) for i in range(count) if 0 <= i + by < count]
    return lax.ppermute(array, axis, pairs)


def product(left, right):
    return jnp.matmul(left, right, precision=highest, preferred_element_type=jnp.float32)


def layer_forward(hidden, matrix, bias, gain, shift, adjacency, rim_below, rim_above, node_count):
    halo_rows = rim_below.shape[0]
    rows_dev = hidden.shape[0]
    padded = extended(hidden, (("rows", 0),), halo_rows)
    padded = jnp.concatenate(
        [
            padded[:halo_rows] * rim_below,
            padded[halo_rows : halo_rows + rows_dev],
            padded[halo_rows + rows_dev :] * rim_above,
        ],
        0,
    )
    joined = jnp.concatenate([hidden, product(adjacency, padded)], 1)
    pre = product(joined, matrix) + bias
    active = jnp.maximum(pre, 0.0)
    totals = lax.psum((jnp.sum(active, 0), jnp.sum(active * active, 0)), "rows")
    mean = totals[0] / node_count
    inverse = lax.rsqrt(totals[1] / node_count - mean * mean + norm_epsilon)
    normed = (active - mean) * inverse
    return (gain * normed + shift, (joined, pre, normed, inverse))


def layer_backward(grad_out, kept, matrix, gain, adjacency, rim_below, rim_above, node_count):
    joined, pre, normed, inverse = kept
    halo_rows = rim_below.shape[0]
    rows_dev = joined.shape[0]
    width = matrix.shape[1]
    grad_gain = jnp.sum(grad_out * normed, 0)
    grad_shift = jnp.sum(grad_out, 0)
    grad_normed = grad_out * gain
    totals = lax.psum((jnp.sum(grad_normed, 0), jnp.sum(grad_normed * normed, 0)), "rows")
    grad_active = inverse * (
        grad_normed - totals[0] / node_count - normed * (totals[1] / node_count)
    )
    grad_pre = jnp.where(pre > 0.0, grad_active, 0.0)
    grad_matrix = product(joined.T, grad_pre)
    grad_bias = jnp.sum(grad_pre, 0)
    grad_joined = product(grad_pre, matrix.T)
    grad_padded = product(adjacency.T, grad_joined[:, width:])
    from_above = passed_along(grad_padded[:halo_rows] * rim_below, "rows", -1)
    from_below = passed_along(grad_padded[halo_rows + rows_dev :] * rim_above, "rows", 1)
    grad_hidden = grad_joined[:, :width] + grad_padded[halo_rows : halo_rows + rows_dev]
    grad_hidden = grad_hidden + jnp.pad(from_above, ((rows_dev - halo_rows, 0), (0, 0)))
    grad_hidden = grad_hidden + jnp.pad(from_below, ((0, rows_dev - halo_rows), (0, 0)))
    return (grad_hidden, grad_matrix, grad_bias, grad_gain, grad_shift)


def gram_sums(shards):
    parts = tuple((product(piece, jnp.swapaxes(piece, -1, -2)) for piece in shards))
    return lax.psum(parts, "batch")


def polish(shards, grams):
    return tuple(
        (
            newton_a * piece + product(newton_b * gram + newton_c * product(gram, gram), piece)
            for piece, gram in zip(shards, grams)
        )
    )


def adamw(param, grad, first, second, count):
    first = adam_first_decay * first + (1.0 - adam_first_decay) * grad
    second = adam_second_decay * second + (1.0 - adam_second_decay) * grad * grad
    first_hat = first / (1.0 - jnp.power(adam_first_decay, count))
    second_hat = second / (1.0 - jnp.power(adam_second_decay, count))
    param = param - adam_rate * (
        first_hat / (jnp.sqrt(second_hat) + adam_epsilon) + adam_shrink * param
    )
    return (param, first, second)


def per_device(
    features,
    edge_rows,
    edge_weight,
    halo_counts,
    labels,
    pair_rows,
    step,
    w_in,
    w_conv,
    w_head,
    biases,
    norm_params,
    head_bias,
    mom_in,
    mom_conv,
    mom_head,
    first_bias,
    first_norm,
    first_head,
    second_bias,
    second_norm,
    second_head,
):
    full_in, full_conv, full_head = (
        lax.all_gather(w_in, "batch", axis=1, tiled=True),
        lax.all_gather(w_conv, "batch", axis=1, tiled=True),
        lax.all_gather(w_head, "batch", axis=0, tiled=True),
    )
    inputs = features[0]
    rows_dev = inputs.shape[0]
    halo_rows = rows_dev // 4
    layers = full_conv.shape[0]
    node_count = rows_dev * lax.axis_size("rows")
    all_nodes = node_count * lax.axis_size("batch")
    edges = edge_rows[0, 0]
    counts = halo_counts[0, 0]
    adjacency = (
        jnp.zeros((rows_dev, rows_dev + 2 * halo_rows), jnp.float32)
        .at[edges[0], edges[1]]
        .add(edge_weight[0, 0])
    )
    place = jnp.arange(halo_rows, dtype=jnp.int32)
    rim_below = (place >= halo_rows - counts[0]).astype(jnp.float32)[:, None]
    rim_above = (place < counts[1]).astype(jnp.float32)[:, None]
    hidden = product(inputs, full_in) + biases[0]
    kept_all = []
    for layer in range(layers):
        hidden, kept = layer_forward(
            hidden,
            full_conv[layer],
            biases[layer + 1],
            norm_params[layer, 0],
            norm_params[layer, 1],
            adjacency,
            rim_below,
            rim_above,
            node_count,
        )
        kept_all.append(kept)
    logits = product(hidden, full_head) + head_bias
    log_total = jax.nn.logsumexp(logits, axis=1)
    classes = logits.shape[1]
    onehot = (labels[0][:, None] == jnp.arange(classes, dtype=jnp.int32)[None, :]).astype(
        jnp.float32
    )
    cross = jnp.sum(log_total) - jnp.sum(onehot * logits)
    picks = pair_rows[0, 0]
    sent = logits[picks]
    received = lax.all_to_all(sent, "rows", split_axis=0, concat_axis=0, tiled=True)
    gap = sent - received
    local_total = cross + pair_weight * jnp.sum(gap * gap)
    grad_logits = jnp.exp(logits - log_total[:, None]) - onehot
    grad_logits = grad_logits.at[picks].add(4.0 * pair_weight * gap)
    grad_logits = grad_logits / all_nodes
    grad_head = product(hidden.T, grad_logits)
    grad_head_bias = jnp.sum(grad_logits, 0)
    grad_hidden = product(grad_logits, full_head.T)
    conv_grads = [None] * layers
    bias_grads = [None] * layers
    norm_grads = [None] * layers
    for layer in reversed(range(layers)):
        grad_hidden, grad_matrix, grad_bias, grad_gain, grad_shift = layer_backward(
            grad_hidden,
            kept_all[layer],
            full_conv[layer],
            norm_params[layer, 0],
            adjacency,
            rim_below,
            rim_above,
            node_count,
        )
        conv_grads[layer] = grad_matrix
        bias_grads[layer] = grad_bias
        norm_grads[layer] = jnp.stack([grad_gain, grad_shift])
    grad_in = product(inputs.T, grad_hidden)
    grad_biases = jnp.stack([jnp.sum(grad_hidden, 0)] + bias_grads)
    grad_norms = jnp.stack(norm_grads)
    grad_conv = jnp.stack(conv_grads)
    summed = lax.psum(
        (grad_in, grad_conv, grad_head, grad_biases, grad_norms, grad_head_bias, local_total),
        ("batch", "rows"),
    )
    shard_index = lax.axis_index("batch")
    shard_in = lax.dynamic_slice_in_dim(summed[0], shard_index * w_in.shape[1], w_in.shape[1], 1)
    shard_conv = lax.dynamic_slice_in_dim(
        summed[1], shard_index * w_conv.shape[1], w_conv.shape[1], 1
    )
    shard_head = lax.dynamic_slice_in_dim(
        summed[2], shard_index * w_head.shape[0], w_head.shape[0], 0
    )
    small = (summed[3], summed[4], summed[5], summed[6])
    moment_in = muon_decay * mom_in + shard_in
    moment_conv = muon_decay * mom_conv + shard_conv
    moment_head = muon_decay * mom_head + shard_head
    shards = (moment_in, jnp.swapaxes(moment_conv, 1, 2), moment_head.T)
    squares = lax.psum(
        (
            jnp.sum(shards[0] * shards[0]),
            jnp.sum(shards[1] * shards[1], axis=(1, 2)),
            jnp.sum(shards[2] * shards[2]),
        ),
        "batch",
    )
    divisors = (
        jnp.sqrt(squares[0]) + 1e-07,
        (jnp.sqrt(squares[1]) + 1e-07)[:, None, None],
        jnp.sqrt(squares[2]) + 1e-07,
    )
    shards = tuple((piece / divisor for piece, divisor in zip(shards, divisors)))
    remaining = NS_STEPS
    for repeat in range(remaining):
        shards = polish(shards, gram_sums(shards))
    scale_in = math.sqrt(max(1.0, full_in.shape[1] / full_in.shape[0]))
    scale_conv = math.sqrt(max(1.0, full_conv.shape[2] / full_conv.shape[1]))
    scale_head = math.sqrt(max(1.0, full_head.shape[1] / full_head.shape[0]))
    new_in = w_in - muon_rate * (scale_in * shards[0] + muon_shrink * w_in)
    new_conv = w_conv - muon_rate * (
        scale_conv * jnp.swapaxes(shards[1], 1, 2) + muon_shrink * w_conv
    )
    new_head = w_head - muon_rate * (scale_head * shards[2].T + muon_shrink * w_head)
    count = step[0].astype(jnp.float32)
    new_bias, bias_first, bias_second = adamw(biases, small[0], first_bias, second_bias, count)
    new_norm, norm_first, norm_second = adamw(norm_params, small[1], first_norm, second_norm, count)
    new_hb, head_first, head_second = adamw(head_bias, small[2], first_head, second_head, count)
    loss = small[3] / all_nodes
    return (
        loss,
        new_in,
        new_conv,
        new_head,
        moment_in,
        moment_conv,
        moment_head,
        new_bias,
        new_norm,
        new_hb,
        bias_first,
        norm_first,
        head_first,
        bias_second,
        norm_second,
        head_second,
    )


def solution(mesh):
    in_specs = (
        P("batch", "rows", None),
        P("batch", "rows", None, None),
        P("batch", "rows", None),
        P("batch", "rows", None),
        P("batch", "rows"),
        P("batch", "rows", None, None),
        P(),
        P(None, "batch"),
        P(None, "batch", None),
        P("batch", None),
        P(),
        P(),
        P(),
        P(None, "batch"),
        P(None, "batch", None),
        P("batch", None),
        P(),
        P(),
        P(),
        P(),
        P(),
        P(),
    )
    out_specs = (
        P(),
        P(None, "batch"),
        P(None, "batch", None),
        P("batch", None),
        P(None, "batch"),
        P(None, "batch", None),
        P("batch", None),
        P(),
        P(),
        P(),
        P(),
        P(),
        P(),
        P(),
        P(),
        P(),
    )
    return jax.shard_map(
        per_device, mesh=mesh, in_specs=in_specs, out_specs=out_specs, check_vma=False
    )
```

profile of v0, /device:TPU:0, one launch (start us, length us, event | category | flops | bytes accessed | tf_op | source)
XLA Modules:
  0.0 1072.4 jit_solution(11864482979756781462)
XLA Ops:
  8.8 6.7 all_gather.9
  15.5 3.1 convolution_add_fusion
  19.6 3.8 collective-permute-start
  27.4 96.1 %scatter_custom_fusion.1 = f32[6291456]{0:T(1024)} fusion(s32[16384]{0:T(1024)S(1)} %broadcast_select_fusion, f32[16384]{0:T(1024)} %bitcast.252, f32[]{:T(128)} %constant.31.clone.1), kind=kCustom, calls=%fused_computation.3 | custom fusion | flops 16384 | bytes 25166336
  123.5 27.1 %reshape.180 = f32[2048,3072]{1,0:T(8,128)} reshape(f32[6291456]{0:T(1024)} %scatter_custom_fusion.1) | data formatting | bytes 50331648 | tf_op jit(solution)/shard_map/scatter-add | solution.py:166
  151.0 23.9 %fusion.8 = f32[2048,256]{1,0:T(8,128)} fusion(f32[2048,3072]{1,0:T(8,128)} %reshape.180, f32[512,256]{1,0:T(8,128)S(1)} %broadcast_multiply_fusion.2, f32[2048,256]{1,0:T(8,128)S(1)} %convolution_add_fusion, f32[512,256]{1,0:T(8,128)S(1)} %broadcast_multiply_fusion.5), kind=kOutput, calls=%fused_computation.14 | convolution fusion | flops 19328925696 | bytes 30408704 | tf_op jit(solution)/shard_map/dot_general | solution.py:51
  174.9 6.6 maximum_reduce_fusion.2
  181.5 22.8 %all-reduce.13 = (f32[256]{0:T(256)S(1)}, f32[256]{0:T(256)S(1)}) all-reduce(f32[256]{0:T(256)S(1)} %get-tuple-element.81, f32[256]{0:T(256)S(1)} %get-tuple-element.80), channel_id=1, replica_groups=mesh['batch'=4,'rows'=8] {'rows'}, use_global_device_ids=true, to_apply=%region_4.0 | all-reduce | flops 512 | bytes 4096 | tf_op jit(solution)/shard_map/psum | solution.py:69
  209.4 17.1 %collective-permute-done.2 = f32[512,256]{1,0:T(8,128)S(1)} collective-permute-done((f32[512,256]{1,0:T(8,128)S(1)}, f32[512,256]{1,0:T(8,128)S(1)}, u32[]{:S(2)}, u32[]{:S(2)}) %collective-permute-start.2) | collective-permute-done | bytes 524320 | tf_op jit(solution)/shard_map/ppermute | solution.py:35
  226.8 23.2 %fusion.14 = f32[2048,256]{1,0:T(8,128)S(1)} fusion(f32[2048,3072]{1,0:T(8,128)} %reshape.180, f32[512,256]{1,0:T(8,128)S(1)} %broadcast_multiply_fusion.1, f32[2048,256]{1,0:T(8,128)S(1)} %multiply_add_fusion.2, f32[512,256]{1,0:T(8,128)S(1)} %broadcast_multiply_fusion.4), kind=kOutput, calls=%fused_computation.20 | convolution fusion | flops 19328925696 | bytes 30408704 | tf_op jit(solution)/shard_map/dot_general | solution.py:51
  250.0 6.4 maximum_reduce_fusion.1
  256.4 19.6 %all-reduce.12 = (f32[256]{0:T(256)S(1)}, f32[256]{0:T(256)S(1)}) all-reduce(f32[256]{0:T(256)S(1)} %get-tuple-element.79, f32[256]{0:T(256)S(1)} %get-tuple-element.78), channel_id=1, replica_groups=mesh['batch'=4,'rows'=8] {'rows'}, use_global_device_ids=true, to_apply=%region_8.0 | all-reduce | flops 512 | bytes 4096 | tf_op jit(solution)/shard_map/psum | solution.py:69
  284.6 5.5 all-gather
  290.9 10.0 collective-permute-done.4
  301.2 23.2 %fusion.20 = f32[2048,256]{1,0:T(8,128)S(1)} fusion(f32[2048,3072]{1,0:T(8,128)} %reshape.180, f32[512,256]{1,0:T(8,128)S(1)} %broadcast_multiply_fusion, f32[2048,256]{1,0:T(8,128)S(1)} %copy-done.4, f32[512,256]{1,0:T(8,128)S(1)} %broadcast_multiply_fusion.3), kind=kOutput, calls=%fused_computation.26 | convolution fusion | flops 19328925696 | bytes 30408704 | tf_op jit(solution)/shard_map/dot_general | solution.py:51
  324.5 6.4 maximum_reduce_fusion
  330.8 19.7 %all-reduce.11 = (f32[256]{0:T(256)S(1)}, f32[256]{0:T(256)S(1)}) all-reduce(f32[256]{0:T(256)S(1)} %get-tuple-element.77, f32[256]{0:T(256)S(1)} %get-tuple-element.76), channel_id=1, replica_groups=mesh['batch'=4,'rows'=8] {'rows'}, use_global_device_ids=true, to_apply=%region_12.0 | all-reduce | flops 512 | bytes 4096 | tf_op jit(solution)/shard_map/psum | solution.py:69
  350.6 4.0 fusion.158
  359.6 3.9 all-to-all-start
  366.0 3.9 all-to-all-done
  373.7 5.1 multiply_reduce_fusion
  378.8 17.8 %all-reduce.10 = (f32[256]{0:T(256)S(1)}, f32[256]{0:T(256)S(1)}) all-reduce(f32[256]{0:T(256)S(1)} %get-tuple-element.69, f32[256]{0:T(256)S(1)} %get-tuple-element.70), channel_id=1, replica_groups=mesh['batch'=4,'rows'=8] {'rows'}, use_global_device_ids=true, to_apply=%region_23.0 | all-reduce | flops 512 | bytes 4096 | tf_op jit(solution)/shard_map/psum | solution.py:84
  396.7 3.0 fusion.150
  401.0 4.8 fusion.91
  405.8 44.1 %fusion.39 = f32[3072,256]{1,0:T(8,128)S(1)} fusion(f32[2048,3072]{1,0:T(8,128)} %reshape.180, f32[2048,512]{1,0:T(8,128)S(1)} %fusion.91), kind=kOutput, calls=%fused_computation.50 | convolution fusion | flops 19327352832 | bytes 30408704 | tf_op jit(solution)/shard_map/dot_general | solution.py:51
  453.2 5.5 collective-permute-start.7
  459.7 3.9 fusion.41
  463.7 5.7 collective-permute-done.7
  469.4 4.7 multiply_reduce_fusion.1
  474.1 19.6 %all-reduce.9 = (f32[256]{0:T(256)S(1)}, f32[256]{0:T(256)S(1)}) all-reduce(f32[256]{0:T(256)S(1)} %get-tuple-element.67, f32[256]{0:T(256)S(1)} %get-tuple-element.71), channel_id=1, replica_groups=mesh['batch'=4,'rows'=8] {'rows'}, use_global_device_ids=true, to_apply=%region_27.28 | all-reduce | flops 512 | bytes 4096 | tf_op jit(solution)/shard_map/psum | solution.py:84
  493.7 3.0 fusion.148
  496.7 4.8 fusion.90
  501.5 43.0 %fusion.35 = f32[3072,256]{1,0:T(8,128)S(1)} fusion(f32[2048,3072]{1,0:T(8,128)} %reshape.180, f32[2048,512]{1,0:T(8,128)S(1)} %fusion.90), kind=kOutput, calls=%fused_computation.45 | convolution fusion | flops 19327352832 | bytes 30408704 | tf_op jit(solution)/shard_map/dot_general | solution.py:51
  546.2 5.3 collective-permute-start.9
  551.6 7.7 fusion.49
  559.3 7.9 fusion.48
  567.3 2.2 multiply_reduce_fusion.2
  569.5 17.5 %all-reduce.8 = (f32[256]{0:T(256)S(1)}, f32[256]{0:T(256)S(1)}) all-reduce(f32[256]{0:T(256)S(1)} %get-tuple-element.65, f32[256]{0:T(256)S(1)} %get-tuple-element.72), channel_id=1, replica_groups=mesh['batch'=4,'rows'=8] {'rows'}, use_global_device_ids=true, to_apply=%region_31.32 | all-reduce | flops 512 | bytes 4096 | tf_op jit(solution)/shard_map/psum | solution.py:84
  587.0 3.0 fusion.146
  590.0 4.8 fusion.89
  594.7 44.2 %fusion.31 = f32[3072,256]{1,0:T(8,128)S(1)} fusion(f32[2048,3072]{1,0:T(8,128)} %reshape.180, f32[2048,512]{1,0:T(8,128)S(1)} %fusion.89), kind=kOutput, calls=%fused_computation.40 | convolution fusion | flops 19327352832 | bytes 30408704 | tf_op jit(solution)/shard_map/dot_general | solution.py:51
  640.7 5.0 collective-permute-start.11
  645.7 6.9 fusion.47
  653.9 2.2 collective-permute-done.11
  656.1 2.2 convolution_bitcast_fusion
  658.4 2.6 fusion.139
  661.0 39.9 %all-reduce.6 = (f32[]{:T(128)}, f32[256,47]{0,1:T(8,128)S(1)}, f32[4,256]{1,0:T(4,128)S(1)}, f32[3,2,256]{2,1,0:T(2,128)S(1)}, f32[47]{0:T(128)S(1)}) all-reduce(f32[]{:T(128)S(6)} %add.478, f32[256,47]{0,1:T(8,128)S(1)} %fusion.41, f32[4,256]{1,0:T(4,128)S(1)} %pad_maximum_fusion.23, ...), channel_id=1, replica_groups=mesh['batch'=4,'rows'=8] {'batch','rows'}, use_global_device_ids=true, to_apply=%region_18.0 | all-reduce | flops 14640 | bytes 117120 | tf_op jit(solution)/shard_map/psum | solution.py:225
  701.7 88.7 %all-reduce.37.cloned.1.call-done = (f32[100,256]{1,0:T(8,128)}, f32[3,512,256]{2,1,0:T(8,128)}) async-done(((f32[100,256]{1,0:T(8,128)}, f32[3,512,256]{2,1,0:T(8,128)}), (f32[100,256]{1,0:T(8,128)}, f32[3,512,256]{2,1,0:T(8,128)})) %all-reduce.37.cloned.1.call-update) | async-done | bytes 1675280 | tf_op jit(solution)/shard_map/psum | solution.py:225
  791.9 6.4 all-reduce.19
  800.1 11.8 %all-reduce.18 = (f32[100,100]{1,0:T(8,128)S(1)}, f32[47,47]{1,0:T(8,128)S(1)}) all-reduce(f32[100,100]{1,0:T(8,128)S(1)} %fusion.104, f32[47,47]{1,0:T(8,128)S(1)} %fusion.134), channel_id=1, replica_groups=mesh['batch'=4,'rows'=8] {'batch'}, use_global_device_ids=true, to_apply=%region_35.36 | all-reduce | flops 12209 | bytes 97672 | tf_op jit(solution)/shard_map/psum | solution.py:103
  813.1 11.0 %all-reduce.17 = (f32[100,100]{1,0:T(8,128)S(1)}, f32[47,47]{1,0:T(8,128)S(1)}) all-reduce(f32[100,100]{1,0:T(8,128)S(1)} %fusion.159, f32[47,47]{1,0:T(8,128)S(1)} %fusion.132), channel_id=1, replica_groups=mesh['batch'=4,'rows'=8] {'batch'}, use_global_device_ids=true, to_apply=%region_36.37 | all-reduce | flops 12209 | bytes 97672 | tf_op jit(solution)/shard_map/psum | solution.py:103
  825.4 11.5 %all-reduce.16 = (f32[100,100]{1,0:T(8,128)S(1)}, f32[47,47]{1,0:T(8,128)S(1)}) all-reduce(f32[100,100]{1,0:T(8,128)S(1)} %fusion.160, f32[47,47]{1,0:T(8,128)S(1)} %fusion.165), channel_id=1, replica_groups=mesh['batch'=4,'rows'=8] {'batch'}, use_global_device_ids=true, to_apply=%region_37.38 | all-reduce | flops 12209 | bytes 97672 | tf_op jit(solution)/shard_map/psum | solution.py:103
  838.1 11.3 %all-reduce.15 = (f32[100,100]{1,0:T(8,128)S(1)}, f32[47,47]{1,0:T(8,128)S(1)}) all-reduce(f32[100,100]{1,0:T(8,128)S(1)} %fusion.161, f32[47,47]{1,0:T(8,128)S(1)} %fusion.130), channel_id=1, replica_groups=mesh['batch'=4,'rows'=8] {'batch'}, use_global_device_ids=true, to_apply=%region_38.39 | all-reduce | flops 12209 | bytes 97672 | tf_op jit(solution)/shard_map/psum | solution.py:103
  851.8 11.1 %all-reduce.14 = (f32[100,100]{1,0:T(8,128)S(1)}, f32[3]{0:T(128)S(1)}, f32[47,47]{1,0:T(8,128)S(1)}) all-reduce(f32[100,100]{1,0:T(8,128)S(1)} %fusion.162, f32[3]{0:T(128)S(1)} %get-tuple-element.125, f32[47,47]{1,0:T(8,128)S(1)} %fusion.103), channel_id=1, replica_groups=mesh['batch'=4,'rows'=8] {'batch'}, use_global_device_ids=true, to_apply=%region_39.40 | all-reduce | flops 12212 | bytes 97696 | tf_op jit(solution)/shard_map/psum | solution.py:103
  864.9 33.7 %all-reduce.27.cloned.1.call-done = f32[3,256,256]{2,1,0:T(8,128)} async-done(((f32[3,256,256]{2,1,0:T(8,128)}), f32[3,256,256]{2,1,0:T(8,128)}) %all-reduce.27.cloned.1.call-update) | async-done | bytes 786448 | tf_op jit(solution)/shard_map/psum | solution.py:103
  898.6 2.6 fusion.46
  906.3 32.6 %all-reduce.29.cloned.1.call-done = f32[3,256,256]{2,1,0:T(8,128)} async-done(((f32[3,256,256]{2,1,0:T(8,128)}), f32[3,256,256]{2,1,0:T(8,128)}) %all-reduce.29.cloned.1.call-update) | async-done | bytes 786448 | tf_op jit(solution)/shard_map/psum | solution.py:103
  939.0 2.6 fusion.45
  946.4 32.9 %all-reduce.31.cloned.1.call-done = f32[3,256,256]{2,1,0:T(8,128)} async-done(((f32[3,256,256]{2,1,0:T(8,128)}), f32[3,256,256]{2,1,0:T(8,128)}) %all-reduce.31.cloned.1.call-update) | async-done | bytes 786448 | tf_op jit(solution)/shard_map/psum | solution.py:103
  979.2 2.6 fusion.44
  986.0 33.4 %all-reduce.33.cloned.1.call-done = f32[3,256,256]{2,1,0:T(8,128)} async-done(((f32[3,256,256]{2,1,0:T(8,128)}), f32[3,256,256]{2,1,0:T(8,128)}) %all-reduce.33.cloned.1.call-update) | async-done | bytes 786448 | tf_op jit(solution)/shard_map/psum | solution.py:103
  1019.4 2.6 fusion.43
  1025.8 33.9 %all-reduce.35.cloned.1.call-done = f32[3,256,256]{2,1,0:T(8,128)} async-done(((f32[3,256,256]{2,1,0:T(8,128)}), f32[3,256,256]{2,1,0:T(8,128)}) %all-reduce.35.cloned.1.call-update) | async-done | bytes 786448 | tf_op jit(solution)/shard_map/psum | solution.py:103
  1059.7 2.7 fusion.42
  (287 shorter events, 69.2 us)
Async XLA Ops:
  7.2 167.7 %all-gather.3.cloned.1.call-start = ((), (), s32[]{:S(2)}) async-start(), calls=%async_computation.1 | async-start | bytes 1966080 | tf_op jit(solution)/shard_map/all_gather | solution.py:152
  15.5 9.2 copy-start.27
  15.5 9.4 copy-start.68
  15.5 9.7 copy-start.69
  18.5 6.9 copy-start.67
  19.6 131.1 %collective-permute-start = (f32[512,256]{1,0:T(8,128)}, f32[512,256]{1,0:T(8,128)S(1)}, u32[]{:S(2)}, u32[]{:S(2)}) collective-permute-start(f32[512,256]{1,0:T(8,128)} %get-tuple-element.151), channel_id=1, source_target_pairs={{0,1},{1,2},{2,3},{3,4},{4,5},{5,6},{6,7},{8,9},{9,10},{10,11},{11... | collective-permute-start | bytes 1572872 | tf_op jit(solution)/shard_map/ppermute | solution.py:35
  23.4 127.4 %collective-permute-start.1 = (f32[512,256]{1,0:T(8,128)}, f32[512,256]{1,0:T(8,128)S(1)}, u32[]{:S(2)}, u32[]{:S(2)}) collective-permute-start(f32[512,256]{1,0:T(8,128)} %get-tuple-element.152), channel_id=1, source_target_pairs={{1,0},{2,1},{3,2},{4,3},{5,4},{6,5},{7,6},{9,8},{10,9},{11,10},{12... | collective-permute-start | bytes 1572872 | tf_op jit(solution)/shard_map/ppermute | solution.py:37
  26.7 274.1 %copy-start.28 = (f32[512]{0:T(512)}, f32[512]{0:T(512)S(1)}, u32[]{:S(2)}) copy-start(f32[512]{0:T(512)S(1)} %fusion.109) | copy-start | bytes 6148
  27.4 273.6 %copy-start.30 = (f32[512]{0:T(512)}, f32[512]{0:T(512)S(1)}, u32[]{:S(2)}) copy-start(f32[512]{0:T(512)S(1)} %fusion.110) | copy-start | bytes 6148
  123.5 27.1 %copy-start.39 = (f32[3,2,256]{2,1,0:T(2,128)S(1)}, f32[3,2,256]{2,1,0:T(2,128)}, u32[]{:S(2)}) copy-start(f32[3,2,256]{2,1,0:T(2,128)} %param.33) | copy-start | bytes 18436
  150.6 53.6 %copy-start.41 = (f32[1,1,256]{2,1,0:T(1,128)}, f32[1,1,256]{2,1,0:T(1,128)S(1)}, u32[]{:S(2)}) copy-start(f32[1,1,256]{2,1,0:T(1,128)S(1)} %get-tuple-element.160) | copy-start | bytes 3076
  150.6 125.4 %copy-start.43 = (f32[1,1,256]{2,1,0:T(1,128)}, f32[1,1,256]{2,1,0:T(1,128)S(1)}, u32[]{:S(2)}) copy-start(f32[1,1,256]{2,1,0:T(1,128)S(1)} %get-tuple-element.161) | copy-start | bytes 3076
  150.7 199.9 %copy-start.45 = (f32[1,1,256]{2,1,0:T(1,128)}, f32[1,1,256]{2,1,0:T(1,128)S(1)}, u32[]{:S(2)}) copy-start(f32[1,1,256]{2,1,0:T(1,128)S(1)} %get-tuple-element.157) | copy-start | bytes 3076
  150.7 199.9 %copy-start.62 = (f32[1,1,256]{2,1,0:T(1,128)}, f32[1,1,256]{2,1,0:T(1,128)S(1)}, u32[]{:S(2)}) copy-start(f32[1,1,256]{2,1,0:T(1,128)S(1)} %get-tuple-element.162) | copy-start | bytes 3076
  206.2 43.8 %copy-start.1 = (f32[2048,256]{1,0:T(8,128)}, f32[2048,256]{1,0:T(8,128)S(1)}, u32[]{:S(2)}) copy-start(f32[2048,256]{1,0:T(8,128)S(1)} %multiply_add_fusion.2) | copy-start | bytes 6291460
  206.3 20.2 %collective-permute-start.2 = (f32[512,256]{1,0:T(8,128)S(1)}, f32[512,256]{1,0:T(8,128)S(1)}, u32[]{:S(2)}, u32[]{:S(2)}) collective-permute-start(f32[512,256]{1,0:T(8,128)S(1)} %get-tuple-element.149), channel_id=1, source_target_pairs={{0,1},{1,2},{2,3},{3,4},{4,5},{5,6},{6,7},{8,9},{9,10},{10,11},{11... | collective-permute-start | bytes 1572872 | tf_op jit(solution)/shard_map/ppermute | solution.py:35
  207.7 19.0 %collective-permute-start.3 = (f32[512,256]{1,0:T(8,128)S(1)}, f32[512,256]{1,0:T(8,128)S(1)}, u32[]{:S(2)}, u32[]{:S(2)}) collective-permute-start(f32[512,256]{1,0:T(8,128)S(1)} %get-tuple-element.150), channel_id=1, source_target_pairs={{1,0},{2,1},{3,2},{4,3},{5,4},{6,5},{7,6},{9,8},{10,9},{11,10},{12... | collective-permute-start | bytes 1572872 | tf_op jit(solution)/shard_map/ppermute | solution.py:37
  280.9 19.9 %collective-permute-start.4 = (f32[512,256]{1,0:T(8,128)}, f32[512,256]{1,0:T(8,128)S(1)}, u32[]{:S(2)}, u32[]{:S(2)}) collective-permute-start(f32[512,256]{1,0:T(8,128)} %get-tuple-element.147), channel_id=1, source_target_pairs={{0,1},{1,2},{2,3},{3,4},{4,5},{5,6},{6,7},{8,9},{9,10},{10,11},{11... | collective-permute-start | bytes 1572872 | tf_op jit(solution)/shard_map/ppermute | solution.py:35
  282.4 18.6 %collective-permute-start.5 = (f32[512,256]{1,0:T(8,128)}, f32[512,256]{1,0:T(8,128)S(1)}, u32[]{:S(2)}, u32[]{:S(2)}) collective-permute-start(f32[512,256]{1,0:T(8,128)} %get-tuple-element.148), channel_id=1, source_target_pairs={{1,0},{2,1},{3,2},{4,3},{5,4},{6,5},{7,6},{9,8},{10,9},{11,10},{12... | collective-permute-start | bytes 1572872 | tf_op jit(solution)/shard_map/ppermute | solution.py:37
  283.9 40.5 %copy-start.35 = (s32[32]{0:T(128)}, s32[32]{0:T(128)S(1)}, u32[]{:S(2)}) copy-start(s32[32]{0:T(128)S(1)} %reshape.183) | copy-start | bytes 388
  290.3 60.3 %copy-start.25 = (f32[256,47]{0,1:T(8,128)}, f32[256,47]{0,1:T(8,128)S(1)}, u32[]{:S(2)}) copy-start(f32[256,47]{0,1:T(8,128)S(1)} %reshape.206) | copy-start | bytes 144388
  290.3 10.9 %copy-start.4 = (f32[2048,256]{1,0:T(8,128)S(1)}, f32[2048,256]{1,0:T(8,128)}, u32[]{:S(2)}) copy-start(f32[2048,256]{1,0:T(8,128)} %copy-done.3) | copy-start | bytes 6291460
  324.4 26.1 %copy-start.70 = (f32[47]{0:T(128)S(1)}, f32[47]{0:T(128)}, u32[]{:S(2)}) copy-start(f32[47]{0:T(128)} %param.34) | copy-start | bytes 568
  359.6 10.3 all-to-all-start
  363.5 426.9 %all-reduce.37.cloned.1.call-start = ((), (), s32[]{:S(2)}) async-start(), calls=%async_computation.7 | async-start | bytes 3358720 | tf_op jit(solution)/shard_map/psum | solution.py:225
  373.7 23.0 %copy-start.46 = (f32[1,1,256]{2,1,0:T(1,128)S(1)}, f32[1,1,256]{2,1,0:T(1,128)}, u32[]{:S(2)}) copy-start(f32[1,1,256]{2,1,0:T(1,128)} %copy-done.45) | copy-start | bytes 3076
  373.7 23.0 %copy-start.56 = (f32[256]{0:T(256)S(1)}, f32[256]{0:T(256)}, u32[]{:S(2)}) copy-start(f32[256]{0:T(256)} %copy-done.55) | copy-start | bytes 3076
  373.7 23.0 %copy-start.58 = (f32[256]{0:T(256)S(1)}, f32[256]{0:T(256)}, u32[]{:S(2)}) copy-start(f32[256]{0:T(256)} %copy-done.57) | copy-start | bytes 3076
  405.8 44.2 %copy-start.11 = (f32[2048,512]{1,0:T(8,128)}, f32[2048,512]{1,0:T(8,128)S(1)}, u32[]{:S(2)}) copy-start(f32[2048,512]{1,0:T(8,128)S(1)} %fusion.91) | copy-start | bytes 12582916
  405.8 44.2 %copy-start.29 = (f32[512]{0:T(512)S(1)}, f32[512]{0:T(512)}, u32[]{:S(2)}) copy-start(f32[512]{0:T(512)} %copy-done.28) | copy-start | bytes 6148
  405.8 44.2 %copy-start.31 = (f32[512]{0:T(512)S(1)}, f32[512]{0:T(512)}, u32[]{:S(2)}) copy-start(f32[512]{0:T(512)} %copy-done.30) | copy-start | bytes 6148
  450.0 9.7 copy-start.63
  451.9 11.8 %collective-permute-start.6 = (f32[512,256]{1,0:T(8,128)}, f32[512,256]{1,0:T(8,128)}, u32[]{:S(2)}, u32[]{:S(2)}) collective-permute-start(f32[512,256]{1,0:T(8,128)} %get-tuple-element.145), channel_id=1, source_target_pairs={{1,0},{2,1},{3,2},{4,3},{5,4},{6,5},{7,6},{9,8},{10,9},{11,10},{12... | collective-permute-start | bytes 1572872 | tf_op jit(solution)/shard_map/ppermute | solution.py:47
  453.2 16.2 %collective-permute-start.7 = (f32[512,256]{1,0:T(8,128)}, f32[512,256]{1,0:T(8,128)}, u32[]{:S(2)}, u32[]{:S(2)}) collective-permute-start(f32[512,256]{1,0:T(8,128)} %get-tuple-element.146), channel_id=1, source_target_pairs={{0,1},{1,2},{2,3},{3,4},{4,5},{5,6},{6,7},{8,9},{9,10},{10,11},{11... | collective-permute-start | bytes 1572872 | tf_op jit(solution)/shard_map/ppermute | solution.py:47
  459.4 10.0 copy-start.8
  459.4 10.0 copy-start.44
  459.4 10.0 copy-start.52
  459.4 10.0 copy-start.54
  501.5 50.0 %copy-start.10 = (f32[2048,256]{1,0:T(8,128)S(1)}, f32[2048,256]{1,0:T(8,128)}, u32[]{:S(2)}) copy-start(f32[2048,256]{1,0:T(8,128)} %copy-done.9) | copy-start | bytes 6291460
  501.5 50.0 %copy-start.17 = (f32[2048,256]{1,0:T(8,128)S(1)}, f32[2048,256]{1,0:T(8,128)}, u32[]{:S(2)}) copy-start(f32[2048,256]{1,0:T(8,128)} %copy-done.16) | copy-start | bytes 6291460
  544.5 7.0 copy-start.5
  544.8 22.5 %collective-permute-start.8 = (f32[512,256]{1,0:T(8,128)S(1)}, f32[512,256]{1,0:T(8,128)S(1)}, u32[]{:S(2)}, u32[]{:S(2)}) collective-permute-start(f32[512,256]{1,0:T(8,128)S(1)} %get-tuple-element.143), channel_id=1, source_target_pairs={{1,0},{2,1},{3,2},{4,3},{5,4},{6,5},{7,6},{9,8},{10,9},{11,10},{12... | collective-permute-start | bytes 1572872 | tf_op jit(solution)/shard_map/ppermute | solution.py:47
  546.2 13.1 %copy-start.2 = (f32[2048,256]{1,0:T(8,128)S(1)}, f32[2048,256]{1,0:T(8,128)}, u32[]{:S(2)}) copy-start(f32[2048,256]{1,0:T(8,128)} %copy-done.1) | copy-start | bytes 6291460
  546.2 13.1 %copy-start.15 = (f32[2048,256]{1,0:T(8,128)S(1)}, f32[2048,256]{1,0:T(8,128)}, u32[]{:S(2)}) copy-start(f32[2048,256]{1,0:T(8,128)} %copy-done.14) | copy-start | bytes 6291460
  546.2 21.0 %collective-permute-start.9 = (f32[512,256]{1,0:T(8,128)S(1)}, f32[512,256]{1,0:T(8,128)S(1)}, u32[]{:S(2)}, u32[]{:S(2)}) collective-permute-start(f32[512,256]{1,0:T(8,128)S(1)} %get-tuple-element.144), channel_id=1, source_target_pairs={{0,1},{1,2},{2,3},{3,4},{4,5},{5,6},{6,7},{8,9},{9,10},{10,11},{11... | collective-permute-start | bytes 1572872 | tf_op jit(solution)/shard_map/ppermute | solution.py:47
  559.3 8.0 copy-start.7
  559.3 8.0 copy-start.42
  559.3 8.0 copy-start.48
  559.3 8.0 copy-start.50
  594.7 61.4 %copy-start = (f32[2048,512]{1,0:T(8,128)}, f32[2048,512]{1,0:T(8,128)S(1)}, u32[]{:S(2)}) copy-start(f32[2048,512]{1,0:T(8,128)S(1)} %fusion.89) | copy-start | bytes 12582916
  638.9 17.2 %copy-start.6 = (f32[3072,256]{1,0:T(8,128)}, f32[3072,256]{1,0:T(8,128)S(1)}, u32[]{:S(2)}) copy-start(f32[3072,256]{1,0:T(8,128)S(1)} %fusion.31) | copy-start | bytes 9437188
  639.1 14.8 %collective-permute-start.10 = (f32[512,256]{1,0:T(8,128)S(1)}, f32[512,256]{1,0:T(8,128)S(1)}, u32[]{:S(2)}, u32[]{:S(2)}) collective-permute-start(f32[512,256]{1,0:T(8,128)S(1)} %get-tuple-element.141), channel_id=1, source_target_pairs={{1,0},{2,1},{3,2},{4,3},{5,4},{6,5},{7,6},{9,8},{10,9},{11,10},{12... | collective-permute-start | bytes 1572872 | tf_op jit(solution)/shard_map/ppermute | solution.py:47
  640.7 15.4 %collective-permute-start.11 = (f32[512,256]{1,0:T(8,128)S(1)}, f32[512,256]{1,0:T(8,128)S(1)}, u32[]{:S(2)}, u32[]{:S(2)}) collective-permute-start(f32[512,256]{1,0:T(8,128)S(1)} %get-tuple-element.142), channel_id=1, source_target_pairs={{0,1},{1,2},{2,3},{3,4},{4,5},{5,6},{6,7},{8,9},{9,10},{10,11},{11... | collective-permute-start | bytes 1572872 | tf_op jit(solution)/shard_map/ppermute | solution.py:47
  658.3 240.3 %all-reduce.27.cloned.1.call-start = ((), (), s32[]{:S(2)}) async-start(), calls=%async_computation.2 | async-start | bytes 1572864 | tf_op jit(solution)/shard_map/psum | solution.py:103
  658.4 42.6 %copy-start.38 = (f32[64,47]{0,1:T(8,128)S(1)}, f32[64,47]{0,1:T(8,128)}, u32[]{:S(2)}) copy-start(f32[64,47]{0,1:T(8,128)} %param.37) | copy-start | bytes 36100
  658.4 132.0 %copy-start.24 = (f32[100,64]{1,0:T(8,128)S(1)}, f32[100,64]{1,0:T(8,128)}, u32[]{:S(2)}) copy-start(f32[100,64]{1,0:T(8,128)} %copy.118) | copy-start | bytes 76804
  661.0 189.7 %copy-start.23 = (f32[3,128,256]{2,1,0:T(8,128)S(1)}, f32[3,128,256]{2,1,0:T(8,128)}, u32[]{:S(2)}) copy-start(f32[3,128,256]{2,1,0:T(8,128)} %param.36) | copy-start | bytes 1179652
  701.7 323.3 %copy-start.32 = (f32[64,47]{0,1:T(8,128)}, f32[64,47]{0,1:T(8,128)S(1)}, u32[]{:S(2)}) copy-start(f32[64,47]{0,1:T(8,128)S(1)} %get-tuple-element.128) | copy-start | bytes 36100
  851.8 210.5 %copy-start.18 = (f32[3,128,256]{2,1,0:T(8,128)}, f32[3,128,256]{2,1,0:T(8,128)S(1)}, u32[]{:S(2)}) copy-start(f32[3,128,256]{2,1,0:T(8,128)S(1)} %get-tuple-element.126) | copy-start | bytes 1179652
  864.8 74.1 %all-reduce.29.cloned.1.call-start = ((), (), s32[]{:S(2)}) async-start(), calls=%async_computation.3 | async-start | bytes 1572864 | tf_op jit(solution)/shard_map/psum | solution.py:103
  904.1 75.1 %all-reduce.31.cloned.1.call-start = ((), (), s32[]{:S(2)}) async-start(), calls=%async_computation.4 | async-start | bytes 1572864 | tf_op jit(solution)/shard_map/psum | solution.py:103
  944.4 75.0 %all-reduce.33.cloned.1.call-start = ((), (), s32[]{:S(2)}) async-start(), calls=%async_computation.5 | async-start | bytes 1572864 | tf_op jit(solution)/shard_map/psum | solution.py:103
  984.6 75.1 %all-reduce.35.cloned.1.call-start = ((), (), s32[]{:S(2)}) async-start(), calls=%async_computation.6 | async-start | bytes 1572864 | tf_op jit(solution)/shard_map/psum | solution.py:103
  1024.8 37.6 %copy-start.22 = (f32[3,128,256]{2,1,0:T(8,128)S(1)}, f32[3,128,256]{2,1,0:T(8,128)}, u32[]{:S(2)}) copy-start(f32[3,128,256]{2,1,0:T(8,128)} %param.30) | copy-start | bytes 1179652
  (30 other events, 113.1 us)
Sparse Core Ops, SparseCore 0:
  9.6 22.3 all-gather.2
  658.5 131.9 all-reduce.36
  865.0 33.6 all-reduce.26
  904.3 34.6 all-reduce.28
  944.5 34.6 all-reduce.30
  984.7 34.6 all-reduce.32
  1024.9 34.7 all-reduce.34
where the time goes:
time: 1080 us; the launch traced here: 1070 us
  matrix products  310 us (29%)
  waiting for transfers between devices  295 us (27%)
  blocking collectives  232 us (21%)
  other arithmetic  137 us (13%)
  local copies, waits for them, and re-layouts  40 us (4%)
  starting transfers between devices  35.3 us (3%)
  between operations  22.5 us (2%)
    dot_general x65, matrix products, product(): jnp.matmul(left, right, precision=highest, preferred_element_type=jnp.flo...  310 us
    psum x5, waiting for transfers between devices, gram_sums(): return lax.psum(parts, 'batch')  166 us
    unnamed x4, other arithmetic  96.7 us
    psum x1, waiting for transfers between devices, per_device(): lax.psum((grad_in, grad_conv, grad_head, grad_biases, grad_norms, grad_he...  88.7 us
    psum x3, blocking collectives, layer_forward(): totals = lax.psum((jnp.sum(active, 0), jnp.sum(active * active, 0)), 'rows')  62.1 us
    psum x5, blocking collectives, gram_sums(): return lax.psum(parts, 'batch')  56.7 us
    psum x3, blocking collectives, layer_backward(): lax.psum((jnp.sum(grad_normed, 0), jnp.sum(grad_normed * normed, 0)), 'ro...  54.9 us
    psum x1, blocking collectives, per_device(): lax.psum((grad_in, grad_conv, grad_head, grad_biases, grad_norms, grad_he...  39.9 us
  transfers between devices with their start and end apart: 20, of which 11 were waited for; matrix products, arithmetic and copies ran while one was open for 18% of the time, Pallas kernels for 0%

commit v1 on v0

v1 whole, which is shorter than its diff:
```python
import functools
import math

import jax
import jax.numpy as jnp
from jax import lax
from jax.experimental import pallas as pl
from jax.experimental.pallas import tpu as pltpu
from jax.sharding import PartitionSpec as P

NS_STEPS = 5

f32 = jnp.float32
highest = lax.Precision.HIGHEST
three_pass = lax.Precision.HIGH
norm_epsilon = 1e-05
pair_weight = 0.05
newton_a = 3.4445
newton_b = -4.775
newton_c = 2.0315
muon_decay = 0.9
muon_rate = 0.5
muon_shrink = 0.01
adam_first_decay = 0.9
adam_second_decay = 0.999
adam_epsilon = 1e-08
adam_rate = 0.1
adam_shrink = 0.01


def product(left, right):
    return jnp.matmul(left, right, precision=highest, preferred_element_type=f32)


def product3(left, right):
    return jnp.matmul(left, right, precision=three_pass, preferred_element_type=f32)


def swap(b, r):
    return 2 * (b // 2) + r % 2, 2 * (r // 2) + b % 2


def flat_pairs(n_batch, n_rows, move):
    pairs = []
    for b in range(n_batch):
        for r in range(n_rows):
            to = move(b, r)
            if to is not None:
                pairs.append((b * n_rows + r, to[0] * n_rows + to[1]))
    return pairs


def redeal(array, n_batch, n_rows):
    return lax.ppermute(array, ("batch", "rows"), flat_pairs(n_batch, n_rows, swap))


def pass_rows(array, n_batch, n_rows, by):
    def move(b, r):
        batch, block = swap(b, r)
        block = block + by
        return swap(batch, block) if 0 <= block < n_rows else None

    return lax.ppermute(array, ("batch", "rows"), flat_pairs(n_batch, n_rows, move))


def peer_place(batch, block):
    two = jnp.int32(2)
    return (
        two * lax.div(batch, two) + lax.rem(block, two),
        two * lax.div(block, two) + lax.rem(batch, two),
    )


def my_place():
    return peer_place(lax.axis_index("batch"), lax.axis_index("rows"))


def greet(n, batch, block):
    barrier = pltpu.get_barrier_semaphore()
    for k in range(1, n):
        pl.semaphore_signal(
            barrier,
            inc=1,
            device_id=peer_place(batch, lax.rem(block + k, n)),
            device_id_type=pl.DeviceIdType.MESH,
        )
    pl.semaphore_wait(barrier, n - 1)


def group_sum_kernel(n, x_ref, o_ref, held, send_sem, recv_sem):
    batch, block = my_place()
    greet(n, batch, block)
    held[0] = x_ref[...]
    copies = []
    for k in range(1, n):
        copy = pltpu.make_async_remote_copy(
            src_ref=x_ref,
            dst_ref=held.at[k],
            send_sem=send_sem.at[k],
            recv_sem=recv_sem.at[k],
            device_id=peer_place(batch, lax.rem(block + k, n)),
            device_id_type=pl.DeviceIdType.MESH,
        )
        copy.start()
        copies.append(copy)
    for copy in copies:
        copy.wait()
    total = held[lax.rem(block, n)]
    for q in range(1, n):
        total = total + held[lax.rem(block + n - q, n)]
    o_ref[...] = total


def group_sum(x, n):
    return pl.pallas_call(
        functools.partial(group_sum_kernel, n),
        out_shape=jax.ShapeDtypeStruct(x.shape, f32),
        in_specs=[pl.BlockSpec(memory_space=pltpu.VMEM)],
        out_specs=pl.BlockSpec(memory_space=pltpu.VMEM),
        scratch_shapes=[
            pltpu.VMEM((n,) + x.shape, f32),
            pltpu.SemaphoreType.DMA((n,)),
            pltpu.SemaphoreType.DMA((n,)),
        ],
        compiler_params=pltpu.CompilerParams(collective_id=1, has_side_effects=True),
        name="group_sum",
    )(x)


def group_gather_kernel(n, x_ref, o_ref, send_sem, recv_sem):
    batch, block = my_place()
    greet(n, batch, block)
    copies = []
    for k in range(1, n):
        peer = lax.rem(block + k, n)
        copy = pltpu.make_async_remote_copy(
            src_ref=x_ref.at[peer],
            dst_ref=o_ref.at[k],
            send_sem=send_sem.at[k],
            recv_sem=recv_sem.at[k],
            device_id=peer_place(batch, peer),
            device_id_type=pl.DeviceIdType.MESH,
        )
        copy.start()
        copies.append(copy)
    o_ref[0] = x_ref[block]
    for copy in copies:
        copy.wait()


def group_gather(x, n):
    return pl.pallas_call(
        functools.partial(group_gather_kernel, n),
        out_shape=jax.ShapeDtypeStruct(x.shape, f32),
        in_specs=[pl.BlockSpec(memory_space=pltpu.VMEM)],
        out_specs=pl.BlockSpec(memory_space=pltpu.VMEM),
        scratch_shapes=[pltpu.SemaphoreType.DMA((n,)), pltpu.SemaphoreType.DMA((n,))],
        compiler_params=pltpu.CompilerParams(collective_id=2, has_side_effects=True),
        name="pair_exchange",
    )(x)


def kdot(left, right, dims=((1,), (0,))):
    return lax.dot_general(left, right, (dims, ((), ())), precision=highest, preferred_element_type=f32)


def muon_kernel(scale_in, scale_head, conv_mom, in_mom, head_mom, conv_q, in_q, head_q, gram_c, poly_c, gram_s, poly_s):
    layers = conv_mom.shape[0]
    for which in range(layers):
        m = conv_mom[which]
        size = jnp.sqrt(jnp.sum(m * m)) + 1e-07
        gram_c[which] = kdot(m, m, ((0,), (0,))) / (size * size)
    m = in_mom[...]
    size = jnp.sqrt(jnp.sum(m * m)) + 1e-07
    gram_s[0] = kdot(m, m, ((1,), (1,))) / (size * size)
    in_size = size
    m = head_mom[...]
    head_size = jnp.sqrt(jnp.sum(m * m)) + 1e-07
    gram_s[1] = kdot(m, m, ((1,), (1,))) / (head_size * head_size)

    def eye(n):
        return (lax.broadcasted_iota(jnp.int32, (n, n), 0) == lax.broadcasted_iota(jnp.int32, (n, n), 1)).astype(f32)

    for which in range(layers):
        poly_c[which] = eye(poly_c.shape[1])
    for which in range(2):
        poly_s[which] = eye(poly_s.shape[1])

    def step(grams, polys):
        n = grams.shape[1]
        count = grams.shape[0]
        a1 = [grams[i] for i in range(count)]
        a2 = [kdot(a, a) for a in a1]
        p = [newton_a * eye(n) + newton_b * x + newton_c * y for x, y in zip(a1, a2)]
        pa = [kdot(x, y) for x, y in zip(p, a1)]
        q = [kdot(x, polys[i]) for i, x in enumerate(p)]
        nxt = [kdot(x, y) for x, y in zip(pa, p)]
        for i in range(count):
            polys[i] = q[i]
            grams[i] = nxt[i]

    def body(_, carry):
        step(gram_c, poly_c)
        step(gram_s, poly_s)
        return carry

    lax.fori_loop(0, NS_STEPS, body, 0)
    for which in range(layers):
        m = conv_mom[which]
        size = jnp.sqrt(jnp.sum(m * m)) + 1e-07
        conv_q[which] = poly_c[which] / size
    in_q[...] = poly_s[0] / in_size * scale_in
    head_q[...] = poly_s[1] / head_size * scale_head


def muon_factors(conv_mom, in_mom, head_mom, scale_in, scale_head):
    layers, _, hid = conv_mom.shape
    small = 128
    in_pad = jnp.pad(in_mom, ((0, small - in_mom.shape[0]), (0, 0)))
    head_t = jnp.pad(head_mom.T, ((0, small - head_mom.shape[1]), (0, 0)))
    return pl.pallas_call(
        functools.partial(muon_kernel, scale_in, scale_head),
        out_shape=(
            jax.ShapeDtypeStruct((layers, hid, hid), f32),
            jax.ShapeDtypeStruct((small, small), f32),
            jax.ShapeDtypeStruct((small, small), f32),
        ),
        in_specs=[pl.BlockSpec(memory_space=pltpu.VMEM)] * 3,
        out_specs=(pl.BlockSpec(memory_space=pltpu.VMEM),) * 3,
        scratch_shapes=[
            pltpu.VMEM((layers, hid, hid), f32),
            pltpu.VMEM((layers, hid, hid), f32),
            pltpu.VMEM((2, small, small), f32),
            pltpu.VMEM((2, small, small), f32),
        ],
        compiler_params=pltpu.CompilerParams(vmem_limit_bytes=40 << 20),
        name="muon",
    )(conv_mom, in_pad, head_t)


def layer_forward(hidden, matrix, bias, gain, shift, adjacency, rim_below, rim_above, node_count, dims):
    halo_rows = rim_below.shape[0]
    rows_dev = hidden.shape[0]
    below = pass_rows(hidden[rows_dev - halo_rows :], *dims, 1)
    above = pass_rows(hidden[:halo_rows], *dims, -1)
    padded = jnp.concatenate([below * rim_below, hidden, above * rim_above], 0)
    joined = jnp.concatenate([hidden, product(adjacency, padded)], 1)
    pre = product(joined, matrix) + bias
    active = jnp.maximum(pre, 0.0)
    totals = group_sum(jnp.stack([jnp.sum(active, 0), jnp.sum(active * active, 0)]), dims[1])
    mean = totals[0] / node_count
    inverse = lax.rsqrt(totals[1] / node_count - mean * mean + norm_epsilon)
    normed = (active - mean) * inverse
    return (gain * normed + shift, (joined, pre, normed, inverse))


def layer_backward(grad_out, kept, matrix, gain, adjacency, rim_below, rim_above, node_count, dims):
    joined, pre, normed, inverse = kept
    halo_rows = rim_below.shape[0]
    rows_dev = joined.shape[0]
    width = matrix.shape[1]
    grad_gain = jnp.sum(grad_out * normed, 0)
    grad_shift = jnp.sum(grad_out, 0)
    totals = group_sum(jnp.stack([grad_shift, grad_gain]), dims[1]) * gain
    grad_normed = grad_out * gain
    grad_active = inverse * (
        grad_normed - totals[0] / node_count - normed * (totals[1] / node_count)
    )
    grad_pre = jnp.where(pre > 0.0, grad_active, 0.0)
    grad_matrix = product3(joined.T, grad_pre)
    grad_bias = jnp.sum(grad_pre, 0)
    grad_joined = product3(grad_pre, matrix.T)
    grad_padded = product3(adjacency.T, grad_joined[:, width:])
    from_above = pass_rows(grad_padded[:halo_rows] * rim_below, *dims, -1)
    from_below = pass_rows(grad_padded[halo_rows + rows_dev :] * rim_above, *dims, 1)
    grad_hidden = grad_joined[:, :width] + grad_padded[halo_rows : halo_rows + rows_dev]
    grad_hidden = grad_hidden + jnp.pad(from_above, ((rows_dev - halo_rows, 0), (0, 0)))
    grad_hidden = grad_hidden + jnp.pad(from_below, ((0, rows_dev - halo_rows), (0, 0)))
    return (grad_hidden, grad_matrix, grad_bias, grad_gain, grad_shift)


def adamw(param, grad, first, second, count):
    first = adam_first_decay * first + (1.0 - adam_first_decay) * grad
    second = adam_second_decay * second + (1.0 - adam_second_decay) * grad * grad
    first_hat = first / (1.0 - jnp.power(adam_first_decay, count))
    second_hat = second / (1.0 - jnp.power(adam_second_decay, count))
    param = param - adam_rate * (
        first_hat / (jnp.sqrt(second_hat) + adam_epsilon) + adam_shrink * param
    )
    return (param, first, second)


def per_device(
    n_batch,
    n_rows,
    features,
    edge_rows,
    edge_weight,
    halo_counts,
    labels,
    pair_rows,
    step,
    w_in,
    w_conv,
    w_head,
    biases,
    norm_params,
    head_bias,
    mom_in,
    mom_conv,
    mom_head,
    first_bias,
    first_norm,
    first_head,
    second_bias,
    second_norm,
    second_head,
):
    dims = (n_batch, n_rows)
    edge_rows, edge_weight, features, halo_counts, labels, pair_rows = (
        redeal(x, *dims) for x in (edge_rows, edge_weight, features, halo_counts, labels, pair_rows)
    )
    full_in, full_conv, full_head, full_mom_in, full_mom_conv, full_mom_head = (
        lax.all_gather(w_in, "batch", axis=1, tiled=True),
        lax.all_gather(w_conv, "batch", axis=1, tiled=True),
        lax.all_gather(w_head, "batch", axis=0, tiled=True),
        lax.all_gather(mom_in, "batch", axis=1, tiled=True),
        lax.all_gather(mom_conv, "batch", axis=1, tiled=True),
        lax.all_gather(mom_head, "batch", axis=0, tiled=True),
    )
    inputs = features[0]
    rows_dev = inputs.shape[0]
    halo_rows = rows_dev // 4
    layers = full_conv.shape[0]
    node_count = rows_dev * n_rows
    all_nodes = node_count * n_batch
    edges = edge_rows[0, 0]
    counts = halo_counts[0, 0]
    adjacency = (
        jnp.zeros((rows_dev, rows_dev + 2 * halo_rows), f32)
        .at[edges[0], edges[1]]
        .add(edge_weight[0, 0])
    )
    place = jnp.arange(halo_rows, dtype=jnp.int32)
    rim_below = (place >= halo_rows - counts[0]).astype(f32)[:, None]
    rim_above = (place < counts[1]).astype(f32)[:, None]
    hidden = product(inputs, full_in) + biases[0]
    kept_all = []
    for layer in range(layers):
        hidden, kept = layer_forward(
            hidden,
            full_conv[layer],
            biases[layer + 1],
            norm_params[layer, 0],
            norm_params[layer, 1],
            adjacency,
            rim_below,
            rim_above,
            node_count,
            dims,
        )
        kept_all.append(kept)
    logits = product(hidden, full_head) + head_bias
    log_total = jax.nn.logsumexp(logits, axis=1)
    classes = logits.shape[1]
    onehot = (labels[0][:, None] == jnp.arange(classes, dtype=jnp.int32)[None, :]).astype(f32)
    cross = jnp.sum(log_total) - jnp.sum(onehot * logits)
    picks = pair_rows[0, 0]
    sent = logits[picks]
    block = my_place()[1]
    got = group_gather(sent, n_rows)
    received = got[lax.rem(block + n_rows - jnp.arange(n_rows, dtype=jnp.int32), n_rows)]
    gap = sent - received
    local_total = cross + pair_weight * jnp.sum(gap * gap)
    grad_logits = jnp.exp(logits - log_total[:, None]) - onehot
    grad_logits = grad_logits.at[picks].add(4.0 * pair_weight * gap)
    grad_logits = grad_logits / all_nodes
    grad_head = product3(hidden.T, grad_logits)
    grad_head_bias = jnp.sum(grad_logits, 0)
    grad_hidden = product3(grad_logits, full_head.T)
    conv_grads = [None] * layers
    bias_grads = [None] * layers
    norm_grads = [None] * layers
    for layer in reversed(range(layers)):
        grad_hidden, grad_matrix, grad_bias, grad_gain, grad_shift = layer_backward(
            grad_hidden,
            kept_all[layer],
            full_conv[layer],
            norm_params[layer, 0],
            adjacency,
            rim_below,
            rim_above,
            node_count,
            dims,
        )
        conv_grads[layer] = grad_matrix
        bias_grads[layer] = grad_bias
        norm_grads[layer] = jnp.stack([grad_gain, grad_shift])
    grad_in = product3(inputs.T, grad_hidden)
    grad_biases = jnp.stack([jnp.sum(grad_hidden, 0)] + bias_grads)
    grad_norms = jnp.stack(norm_grads)
    grad_conv = jnp.stack(conv_grads)
    summed = lax.psum(
        (grad_in, grad_conv, grad_head, grad_biases, grad_norms, grad_head_bias, local_total),
        ("batch", "rows"),
    )
    small = (summed[3], summed[4], summed[5], summed[6])
    moment_in = muon_decay * full_mom_in + summed[0]
    moment_conv = muon_decay * full_mom_conv + summed[1]
    moment_head = muon_decay * full_mom_head + summed[2]
    scale_in = math.sqrt(max(1.0, full_in.shape[1] / full_in.shape[0]))
    scale_conv = math.sqrt(max(1.0, full_conv.shape[2] / full_conv.shape[1]))
    scale_head = math.sqrt(max(1.0, full_head.shape[1] / full_head.shape[0]))
    conv_q, in_q, head_q = muon_factors(moment_conv, moment_in, moment_head, scale_in, scale_head)
    at = lax.axis_index("batch")
    moment_in = lax.dynamic_slice_in_dim(moment_in, at * w_in.shape[1], w_in.shape[1], 1)
    moment_conv = lax.dynamic_slice_in_dim(moment_conv, at * w_conv.shape[1], w_conv.shape[1], 1)
    moment_head = lax.dynamic_slice_in_dim(moment_head, at * w_head.shape[0], w_head.shape[0], 0)
    feat, classes = w_in.shape[0], w_head.shape[1]
    turn_in = product(in_q[:feat, :feat], moment_in)
    turn_conv = jnp.einsum("lij,ljk->lik", moment_conv, conv_q, precision=highest)
    turn_head = product(moment_head, head_q[:classes, :classes])
    new_in = w_in - muon_rate * (turn_in + muon_shrink * w_in)
    new_conv = w_conv - muon_rate * (scale_conv * turn_conv + muon_shrink * w_conv)
    new_head = w_head - muon_rate * (turn_head + muon_shrink * w_head)
    count = step[0].astype(f32)
    new_bias, bias_first, bias_second = adamw(biases, small[0], first_bias, second_bias, count)
    new_norm, norm_first, norm_second = adamw(norm_params, small[1], first_norm, second_norm, count)
    new_hb, head_first, head_second = adamw(head_bias, small[2], first_head, second_head, count)
    loss = small[3] / all_nodes
    return (
        loss,
        new_in,
        new_conv,
        new_head,
        moment_in,
        moment_conv,
        moment_head,
        new_bias,
        new_norm,
        new_hb,
        bias_first,
        norm_first,
        head_first,
        bias_second,
        norm_second,
        head_second,
    )


def solution(mesh):
    in_specs = (
        P("batch", "rows", None),
        P("batch", "rows", None, None),
        P("batch", "rows", None),
        P("batch", "rows", None),
        P("batch", "rows"),
        P("batch", "rows", None, None),
        P(),
        P(None, "batch"),
        P(None, "batch", None),
        P("batch", None),
        P(),
        P(),
        P(),
        P(None, "batch"),
        P(None, "batch", None),
        P("batch", None),
        P(),
        P(),
        P(),
        P(),
        P(),
        P(),
    )
    out_specs = (
        P(),
        P(None, "batch"),
        P(None, "batch", None),
        P("batch", None),
        P(None, "batch"),
        P(None, "batch", None),
        P("batch", None),
        P(),
        P(),
        P(),
        P(),
        P(),
        P(),
        P(),
        P(),
        P(),
    )
    body = functools.partial(per_device, mesh.shape["batch"], mesh.shape["rows"])
    return jax.shard_map(body, mesh=mesh, in_specs=in_specs, out_specs=out_specs, check_vma=False)
```

time: 1080 us -> 705 us (0.65)
  waiting for transfers between devices: 295 us -> 92 us
  blocking collectives: 232 us -> 76.7 us
  matrix products: 310 us -> 206 us
  Pallas kernels: 0 us -> 84.5 us
    psum x12 -> x0, blocking collectives: 180 us -> none  [the longest x3 62.1 us: layer_forward(): totals = lax.psum((jnp.sum(active, 0), jnp.sum(active * active, 0)), 'rows')]
    psum x5 -> x0, waiting for transfers between devices: 166 us -> none  [gram_sums(): return lax.psum(parts, 'batch')]
    dot_general x65 -> x23, matrix products: 310 us -> 206 us  [the longest x12 107 us: product3(): jnp.matmul(left, right, precision=three_pass, preferred_element_type=f32)]
    pallas_call x0 -> x8, Pallas kernels: none -> 84.5 us  [the longest x6 58.8 us: group_sum(): pl.pallas_call(functools.partial(group_sum_kernel, n), out_shape=jax.Shap...]
    ppermute x12 -> x18, waiting for transfers between devices: 35.1 us -> 4.2 us  [the longest x12 4.18 us: pass_rows(): lax.ppermute(array, ('batch', 'rows'), flat_pairs(n_batch, n_rows, move))]
    psum x1, waiting for transfers between devices: 88.7 us -> 67.8 us  [per_device(): lax.psum((grad_in, grad_conv, grad_head, grad_biases, grad_norms, grad_he...]
    all_gather x0 -> x1, waiting for transfers between devices: none -> 18.6 us  [per_device(): lax.all_gather(mom_conv, 'batch', axis=1, tiled=True)]
    ppermute x12 -> x18, starting transfers between devices: 30.9 us -> 33.1 us  [the longest x12 25.6 us: pass_rows(): lax.ppermute(array, ('batch', 'rows'), flat_pairs(n_batch, n_rows, move))]
  transfers between devices with their start and end apart: 20 -> 21, of which waited for: 11 -> 4; matrix products, arithmetic and copies ran while one was open for 18% -> 36% of each run, Pallas kernels for 0% -> 3%
where the time goes in v1:
time: 705 us; the launch traced here: 696 us
  matrix products  206 us (29%)
  other arithmetic  139 us (20%)
  waiting for transfers between devices  92 us (13%)
  Pallas kernels  84.5 us (12%)
  blocking collectives  76.7 us (11%)
  local copies, waits for them, and re-layouts  44.2 us (6%)
  starting transfers between devices  33.2 us (5%)
  between operations  20.5 us (3%)
    dot_general x12, matrix products, product3(): jnp.matmul(left, right, precision=three_pass, preferred_element_type=f32)  107 us
    dot_general x10, matrix products, product(): jnp.matmul(left, right, precision=highest, preferred_element_type=f32)  97.3 us
    unnamed x4, other arithmetic  97.1 us
    psum x1, waiting for transfers between devices, per_device(): lax.psum((grad_in, grad_conv, grad_head, grad_biases, grad_norms, grad_he...  67.8 us
    pallas_call x6, Pallas kernels, group_sum(): pl.pallas_call(functools.partial(group_sum_kernel, n), out_shape=jax.Shap...  58.8 us
    psum x1, blocking collectives, per_device(): lax.psum((grad_in, grad_conv, grad_head, grad_biases, grad_norms, grad_he...  42.3 us
    scatter-add x1, local copies, waits for them, and re-layouts, per_device(): adjacency = jnp.zeros((rows_dev, rows_dev + 2 * halo_rows), f32).at[edges...  27.2 us
    ppermute x12, starting transfers between devices, pass_rows(): lax.ppermute(array, ('batch', 'rows'), flat_pairs(n_batch, n_rows, move))  25.6 us
  transfers between devices with their start and end apart: 21, of which 4 were waited for; matrix products, arithmetic and copies ran while one was open for 36% of the time, Pallas kernels for 3%

profile of v1, /device:TPU:0, one launch (start us, length us, event | category | flops | bytes accessed | tf_op | source)
XLA Modules:
  0.0 696.0 jit_solution(5700818776104866619)
XLA Ops:
  9.3 1.5 collective-permute-start.2
  10.8 1.6 collective-permute-start.1
  12.3 1.8 collective-permute-start
  15.8 12.3 %all_gather.18 = f32[100,256]{0,1:T(8,128)S(1)} all-gather(f32[100,64]{0,1:T(8,128)} %param.29), channel_id=1, replica_groups=mesh['batch'=4,'rows'=8] {'batch'}, dimensions={1}, use_global_device_ids=true | all-gather | bytes 128000 | tf_op jit(solution)/shard_map/all_gather | solution.py:324
  31.1 1.9 convolution_add_fusion
  34.1 3.2 collective-permute-start.3
  38.9 95.8 %scatter_custom_fusion.1 = f32[6291456]{0:T(1024)} fusion(s32[16384]{0:T(1024)S(1)} %broadcast_select_fusion, f32[16384]{0:T(1024)S(1)} %bitcast.191, f32[]{:T(128)} %constant.31.clone.1), kind=kCustom, calls=%fused_computation.4 | custom fusion | flops 16384 | bytes 25165828
  134.7 27.2 %reshape.201 = f32[2048,3072]{1,0:T(8,128)} reshape(f32[6291456]{0:T(1024)} %scatter_custom_fusion.1) | data formatting | bytes 50331648 | tf_op jit(solution)/shard_map/scatter-add | solution.py:342
  162.2 23.9 %fusion.8 = f32[2048,256]{1,0:T(8,128)} fusion(f32[2048,3072]{1,0:T(8,128)} %reshape.201, f32[512,256]{1,0:T(8,128)S(1)} %broadcast_multiply_fusion.2, f32[2048,256]{1,0:T(8,128)S(1)} %convolution_add_fusion, f32[512,256]{1,0:T(8,128)S(1)} %broadcast_multiply_fusion.5), kind=kOutput, calls=%fused_computation.15 | convolution fusion | flops 19328925696 | bytes 30408704 | tf_op jit(solution)/shard_map/dot_general | solution.py:32
  186.1 6.6 maximum_reduce_fusion.2
  193.3 8.3 %group_sum.6 = f32[2,256]{1,0:T(2,128)} custom-call(f32[2,256]{1,0:T(2,128)} %pad_maximum_fusion.24.x_ref), custom_call_target="tpu_custom_call" | custom-call | tf_op jit(solution)/shard_map/group_sum/pallas_call | solution.py:115
  202.4 1.9 multiply_add_fusion.2
  205.4 2.0 collective-permute-start.6
  210.2 11.3 %all-gather = f32[4,64,47]{1,2,0:T(8,128)S(1)} all-gather(f32[1,64,47]{1,2,0:T(8,128)S(1)} %bitcast.126), channel_id=1, replica_groups=mesh['batch'=4,'rows'=8] {'batch'}, dimensions={0}, use_global_device_ids=true | all-gather | bytes 60160 | tf_op jit(solution)/shard_map/all_gather | solution.py:326
  221.9 23.1 %fusion.14 = f32[2048,256]{1,0:T(8,128)S(1)} fusion(f32[2048,3072]{1,0:T(8,128)} %reshape.201, f32[512,256]{1,0:T(8,128)S(1)} %broadcast_multiply_fusion.1, f32[2048,256]{1,0:T(8,128)S(1)} %multiply_add_fusion.2, f32[512,256]{1,0:T(8,128)S(1)} %broadcast_multiply_fusion.4), kind=kOutput, calls=%fused_computation.21 | convolution fusion | flops 19328925696 | bytes 30408704 | tf_op jit(solution)/shard_map/dot_general | solution.py:32
  245.1 6.4 maximum_reduce_fusion.1
  252.1 7.6 %group_sum.7 = f32[2,256]{1,0:T(2,128)} custom-call(f32[2,256]{1,0:T(2,128)} %pad_maximum_fusion.25.x_ref), custom_call_target="tpu_custom_call" | custom-call | tf_op jit(solution)/shard_map/group_sum/pallas_call | solution.py:115
  260.5 1.9 multiply_add_fusion.1
  263.6 2.0 collective-permute-start.8
  268.4 2.7 collective-permute-done.9
  271.3 23.3 %fusion.20 = f32[2048,256]{1,0:T(8,128)S(1)} fusion(f32[2048,3072]{1,0:T(8,128)} %reshape.201, f32[512,256]{1,0:T(8,128)S(1)} %broadcast_multiply_fusion, f32[2048,256]{1,0:T(8,128)S(1)} %multiply_add_fusion.1, f32[512,256]{1,0:T(8,128)S(1)} %broadcast_multiply_fusion.3), kind=kOutput, calls=%fused_computation.27 | convolution fusion | flops 19328925696 | bytes 30408704 | tf_op jit(solution)/shard_map/dot_general | solution.py:32
  294.6 6.4 maximum_reduce_fusion
  301.6 13.7 %group_sum.8 = f32[2,256]{1,0:T(2,128)} custom-call(f32[2,256]{1,0:T(2,128)} %pad_maximum_fusion.26.x_ref), custom_call_target="tpu_custom_call" | custom-call | tf_op jit(solution)/shard_map/group_sum/pallas_call | solution.py:115
  316.1 4.0 fusion.115
  323.6 2.4 gather_fusion
  326.0 6.9 pair_exchange.1
  332.8 1.4 gather_fusion.1
  334.2 1.9 broadcast_multiply_fusion.7
  337.9 4.5 fusion.99
  343.0 6.8 group_sum.9
  350.5 3.0 fusion.107
  354.9 3.0 fusion.72
  357.8 24.0 %fusion.39 = f32[3072,256]{1,0:T(8,128)S(1)} fusion(f32[2048,3072]{1,0:T(8,128)} %reshape.201, f32[2048,512]{1,0:T(8,128)S(1)} %fusion.72), kind=kOutput, calls=%fused_computation.51 | convolution fusion | flops 9663676416 | bytes 30408704 | tf_op jit(solution)/shard_map/dot_general | solution.py:36
  382.1 1.4 collective-permute-start.12
  383.5 3.1 collective-permute-start.13
  386.6 1.5 collective-permute-done.13
  388.1 2.0 fusion.98
  390.7 13.7 %group_sum.10 = f32[2,256]{1,0:T(2,128)} custom-call(f32[2,256]{1,0:T(2,128)} %get-tuple-element.139.x_ref), custom_call_target="tpu_custom_call" | custom-call | tf_op jit(solution)/shard_map/group_sum/pallas_call | solution.py:115
  405.0 3.0 fusion.105
  409.4 3.0 fusion.71
  412.4 24.0 %fusion.35 = f32[3072,256]{1,0:T(8,128)S(1)} fusion(f32[2048,3072]{1,0:T(8,128)} %reshape.201, f32[2048,512]{1,0:T(8,128)S(1)} %fusion.71), kind=kOutput, calls=%fused_computation.46 | convolution fusion | flops 9663676416 | bytes 30408704 | tf_op jit(solution)/shard_map/dot_general | solution.py:36
  436.6 1.4 collective-permute-start.14
  438.1 3.7 collective-permute-start.15
  441.8 5.9 fusion.44
  447.7 2.0 fusion.97
  450.4 8.7 %group_sum.11 = f32[2,256]{1,0:T(2,128)} custom-call(f32[2,256]{1,0:T(2,128)} %get-tuple-element.137.x_ref), custom_call_target="tpu_custom_call" | custom-call | tf_op jit(solution)/shard_map/group_sum/pallas_call | solution.py:115
  459.8 2.4 fusion.103
  462.1 3.3 fusion.70
  465.5 25.2 %fusion.31 = f32[3072,256]{1,0:T(8,128)S(1)} fusion(f32[2048,3072]{1,0:T(8,128)} %reshape.201, f32[2048,512]{1,0:T(8,128)S(1)} %fusion.70), kind=kOutput, calls=%fused_computation.41 | convolution fusion | flops 9663676416 | bytes 30408704 | tf_op jit(solution)/shard_map/dot_general | solution.py:36
  490.9 1.4 collective-permute-start.16
  492.4 3.5 collective-permute-start.17
  495.9 5.7 fusion.43
  501.7 3.5 fusion.42
  508.1 1.7 convolution_bitcast_fusion
  511.3 5.3 all-gather.1
  516.8 5.4 all_gather.22
  524.3 1.7 multiply_reduce_fusion.6
  526.0 3.0 fusion.41
  529.1 1.7 fusion.95
  530.8 42.3 %all-reduce.8 = (f32[]{:T(128)}, f32[256,47]{0,1:T(8,128)S(1)}, f32[4,256]{1,0:T(4,128)S(1)}, f32[3,2,256]{2,1,0:T(2,128)S(1)}, f32[47]{0:T(128)S(1)}) all-reduce(f32[]{:T(128)S(6)} %add.319, f32[256,47]{0,1:T(8,128)S(1)} %fusion.41, f32[4,256]{1,0:T(4,128)S(1)} %pad_maximum_fusion.23, ...), channel_id=1, replica_groups=mesh['batch'=4,'rows'=8] {'batch','rows'}, use_global_device_ids=true, to_apply=%region_12.0 | all-reduce | flops 14640 | bytes 117120 | tf_op jit(solution)/shard_map/psum | solution.py:403
  575.7 67.8 %all-reduce.12.cloned.1.call-done = (f32[100,256]{1,0:T(8,128)}, f32[3,512,256]{2,1,0:T(8,128)}) async-done(((f32[100,256]{1,0:T(8,128)}, f32[3,512,256]{2,1,0:T(8,128)}), (f32[100,256]{1,0:T(8,128)}, f32[3,512,256]{2,1,0:T(8,128)})) %all-reduce.12.cloned.1.call-update) | async-done | bytes 1675280 | tf_op jit(solution)/shard_map/psum | solution.py:403
  645.3 18.6 %all-gather.7.cloned.1.call-done = f32[3,512,256]{2,1,0:T(8,128)} async-done(((f32[3,128,256]{2,1,0:T(8,128)}), f32[3,512,256]{2,1,0:T(8,128)}) %all-gather.7.cloned.1.call-update) | async-done | bytes 1572880 | tf_op jit(solution)/shard_map/all_gather | solution.py:328
  663.9 2.1 multiply_add_fusion.5.conv_mom
  666.1 18.8 %muon.1 = (f32[3,256,256]{2,1,0:T(8,128)S(1)}, f32[128,128]{1,0:T(8,128)S(1)}, f32[128,128]{1,0:T(8,128)S(1)}) custom-call(f32[3,512,256]{2,1,0:T(8,128)S(1)} %multiply_add_fusion.5.conv_mom, f32[128,256]{1,0:T(8,128)S(1)} %pad.34.in_mom, f32[128,256]{1,0:T(8,128)S(1)} %pad.35.head_mom), custom_call_target="tpu_custom_call" | custom-call | tf_op jit(solution)/shard_map/muon/pallas_call | solution.py:221
  (230 shorter events, 44.3 us)
Async XLA Ops:
  7.2 179.0 %all-gather.5.cloned.1.call-start = ((), (), s32[]{:S(2)}) async-start(), calls=%async_computation | async-start | bytes 1966080 | tf_op jit(solution)/shard_map/all_gather | solution.py:325
  7.9 635.6 %all-reduce.12.cloned.1.call-start = ((), (), s32[]{:S(2)}) async-start(), calls=%async_computation.2 | async-start | bytes 3358720 | tf_op jit(solution)/shard_map/psum | solution.py:403
  8.0 20.1 %collective-permute-start.4 = (s32[1,1,2]{2,1,0:T(1,128)}, s32[1,1,2]{2,1,0:T(1,128)S(1)}, u32[]{:S(2)}, u32[]{:S(2)}) collective-permute-start(s32[1,1,2]{2,1,0:T(1,128)} %param.25), channel_id=1, source_target_pairs={{0,0},{1,8},{2,2},{3,10},{4,4},{5,12},{6,6},{7,14},{8,1},{9,9},{10... | collective-permute-start | bytes 32 | tf_op jit(solution)/shard_map/ppermute | solution.py:54
  9.3 29.6 %collective-permute-start.2 = (f32[1,1,16384]{2,1,0:T(1,128)}, f32[1,1,16384]{2,1,0:T(1,128)S(1)}, u32[]{:S(2)}, u32[]{:S(2)}) collective-permute-start(f32[1,1,16384]{2,1,0:T(1,128)} %param.24), channel_id=1, source_target_pairs={{0,0},{1,8},{2,2},{3,10},{4,4},{5,12},{6,6},{7,14},{8,1},{9,9},{10... | collective-permute-start | bytes 196616 | tf_op jit(solution)/shard_map/ppermute | solution.py:54
  10.8 19.2 %collective-permute-start.1 = (s32[1,1,2,16384]{3,2,1,0:T(2,128)}, s32[1,1,2,16384]{3,2,1,0:T(2,128)S(1)}, u32[]{:S(2)}, u32[]{:S(2)}) collective-permute-start(s32[1,1,2,16384]{3,2,1,0:T(2,128)} %param.23), channel_id=1, source_target_pairs={{0,0},{1,8},{2,2},{3,10},{4,4},{5,12},{6,6},{7,14},{8,1},{9,9},{10... | collective-permute-start | bytes 393224 | tf_op jit(solution)/shard_map/ppermute | solution.py:54
  12.3 18.8 %collective-permute-start = (f32[1,2048,100]{1,0,2:T(1,128)}, f32[1,2048,100]{1,0,2:T(1,128)S(1)}, u32[]{:S(2)}, u32[]{:S(2)}) collective-permute-start(f32[1,2048,100]{1,0,2:T(1,128)} %param.22), channel_id=1, source_target_pairs={{0,0},{1,8},{2,2},{3,10},{4,4},{5,12},{6,6},{7,14},{8,1},{9,9},{10... | collective-permute-start | bytes 2457608 | tf_op jit(solution)/shard_map/ppermute | solution.py:54
  15.7 186.7 %copy-start.46 = (f32[1,1,256]{2,1,0:T(1,128)}, f32[1,1,256]{2,1,0:T(1,128)S(1)}, u32[]{:S(2)}) copy-start(f32[1,1,256]{2,1,0:T(1,128)S(1)} %get-tuple-element.129) | copy-start | bytes 3076
  15.7 244.8 %copy-start.48 = (f32[1,1,256]{2,1,0:T(1,128)}, f32[1,1,256]{2,1,0:T(1,128)S(1)}, u32[]{:S(2)}) copy-start(f32[1,1,256]{2,1,0:T(1,128)S(1)} %get-tuple-element.130) | copy-start | bytes 3076
  15.7 300.3 %copy-start.44 = (f32[1,1,256]{2,1,0:T(1,128)}, f32[1,1,256]{2,1,0:T(1,128)S(1)}, u32[]{:S(2)}) copy-start(f32[1,1,256]{2,1,0:T(1,128)S(1)} %get-tuple-element.126) | copy-start | bytes 3076
  15.7 300.3 %copy-start.54 = (f32[1,1,256]{2,1,0:T(1,128)}, f32[1,1,256]{2,1,0:T(1,128)S(1)}, u32[]{:S(2)}) copy-start(f32[1,1,256]{2,1,0:T(1,128)S(1)} %get-tuple-element.131) | copy-start | bytes 3076
  31.1 6.2 copy-start.58
  33.0 153.1 %copy-start.2 = (f32[2048,256]{1,0:T(8,128)}, f32[2048,256]{1,0:T(8,128)S(1)}, u32[]{:S(2)}) copy-start(f32[2048,256]{1,0:T(8,128)S(1)} %convolution_add_fusion) | copy-start | bytes 6291460
  34.1 127.8 %collective-permute-start.3 = (f32[512,256]{1,0:T(8,128)}, f32[512,256]{1,0:T(8,128)S(1)}, u32[]{:S(2)}, u32[]{:S(2)}) collective-permute-start(f32[512,256]{1,0:T(8,128)} %get-tuple-element.120), channel_id=1, source_target_pairs={{0,8},{1,9},{2,10},{3,11},{4,12},{5,13},{6,14},{7,15},{8,2},{9,3},... | collective-permute-start | bytes 1572872 | tf_op jit(solution)/shard_map/ppermute | solution.py:63
  37.6 124.5 %collective-permute-start.5 = (f32[512,256]{1,0:T(8,128)}, f32[512,256]{1,0:T(8,128)S(1)}, u32[]{:S(2)}, u32[]{:S(2)}) collective-permute-start(f32[512,256]{1,0:T(8,128)} %get-tuple-element.121), channel_id=1, source_target_pairs={{2,8},{3,9},{4,10},{5,11},{6,12},{7,13},{8,0},{9,1},{10,2},{11,3},... | collective-permute-start | bytes 1572872 | tf_op jit(solution)/shard_map/ppermute | solution.py:63
  204.3 40.7 %copy-start.4 = (f32[2048,256]{1,0:T(8,128)}, f32[2048,256]{1,0:T(8,128)S(1)}, u32[]{:S(2)}) copy-start(f32[2048,256]{1,0:T(8,128)S(1)} %multiply_add_fusion.2) | copy-start | bytes 6291460
  205.4 16.2 %collective-permute-start.6 = (f32[512,256]{1,0:T(8,128)}, f32[512,256]{1,0:T(8,128)S(1)}, u32[]{:S(2)}, u32[]{:S(2)}) collective-permute-start(f32[512,256]{1,0:T(8,128)} %get-tuple-element.118), channel_id=1, source_target_pairs={{0,8},{1,9},{2,10},{3,11},{4,12},{5,13},{6,14},{7,15},{8,2},{9,3},... | collective-permute-start | bytes 1572872 | tf_op jit(solution)/shard_map/ppermute | solution.py:63
  207.5 14.3 %collective-permute-start.7 = (f32[512,256]{1,0:T(8,128)}, f32[512,256]{1,0:T(8,128)S(1)}, u32[]{:S(2)}, u32[]{:S(2)}) collective-permute-start(f32[512,256]{1,0:T(8,128)} %get-tuple-element.119), channel_id=1, source_target_pairs={{2,8},{3,9},{4,10},{5,11},{6,12},{7,13},{8,0},{9,1},{10,2},{11,3},... | collective-permute-start | bytes 1572872 | tf_op jit(solution)/shard_map/ppermute | solution.py:63
  208.8 58.7 %collective-permute-start.11 = (s32[1,1,8,4]{2,3,1,0:T(4,128)S(1)}, s32[1,1,8,4]{2,3,1,0:T(4,128)S(1)}, u32[]{:S(2)}, u32[]{:S(2)}) collective-permute-start(s32[1,1,8,4]{2,3,1,0:T(4,128)S(1)} %copy-done.64), channel_id=1, source_target_pairs={{0,0},{1,8},{2,2},{3,10},{4,4},{5,12},{6,6},{7,14},{8,1},{9,9},{10... | collective-permute-start | bytes 392 | tf_op jit(solution)/shard_map/ppermute | solution.py:54
  209.5 112.0 %collective-permute-start.10 = (s32[1,2048]{1,0:T(1,128)S(1)}, s32[1,2048]{1,0:T(1,128)S(1)}, u32[]{:S(2)}, u32[]{:S(2)}) collective-permute-start(s32[1,2048]{1,0:T(1,128)S(1)} %copy-done.63), channel_id=1, source_target_pairs={{0,0},{1,8},{2,2},{3,10},{4,4},{5,12},{6,6},{7,14},{8,1},{9,9},{10... | collective-permute-start | bytes 24584 | tf_op jit(solution)/shard_map/ppermute | solution.py:54
  221.6 94.5 %copy-start.25 = (f32[256,47]{0,1:T(8,128)}, f32[256,47]{0,1:T(8,128)S(1)}, u32[]{:S(2)}) copy-start(f32[256,47]{0,1:T(8,128)S(1)} %reshape.235) | copy-start | bytes 144388
  245.1 6.5 copy-start.16
  263.6 4.7 collective-permute-start.8
  266.2 4.9 collective-permute-start.9
  294.6 6.4 copy-start.17
  294.6 21.5 %copy-start.59 = (f32[47]{0:T(128)S(1)}, f32[47]{0:T(128)}, u32[]{:S(2)}) copy-start(f32[47]{0:T(128)} %param.34) | copy-start | bytes 568
  316.1 7.5 %copy-start.50 = (s32[1024]{0:T(1024)S(1)}, s32[1024]{0:T(1024)}, u32[]{:S(2)}) copy-start(s32[1024]{0:T(1024)} %pad_clamp_fusion.1) | copy-start | bytes 12292
  337.9 11.9 %copy-start.45 = (f32[1,1,256]{2,1,0:T(1,128)S(1)}, f32[1,1,256]{2,1,0:T(1,128)}, u32[]{:S(2)}) copy-start(f32[1,1,256]{2,1,0:T(1,128)} %copy-done.44) | copy-start | bytes 3076
  337.9 12.6 %copy-start.37 = (f32[1,256]{1,0:T(1,128)S(1)}, f32[1,256]{1,0:T(1,128)}, u32[]{:S(2)}) copy-start(f32[1,256]{1,0:T(1,128)} %copy-done.36) | copy-start | bytes 3076
  337.9 12.6 %copy-start.39 = (f32[1,256]{1,0:T(1,128)S(1)}, f32[1,256]{1,0:T(1,128)}, u32[]{:S(2)}) copy-start(f32[1,256]{1,0:T(1,128)} %copy-done.38) | copy-start | bytes 3076
  381.8 6.2 copy-start.8
  381.9 6.2 copy-start.41
  381.9 6.2 copy-start.43
  382.1 4.5 collective-permute-start.12
  383.5 20.8 %copy-start.49 = (f32[1,1,256]{2,1,0:T(1,128)S(1)}, f32[1,1,256]{2,1,0:T(1,128)}, u32[]{:S(2)}) copy-start(f32[1,1,256]{2,1,0:T(1,128)} %copy-done.48) | copy-start | bytes 3076
  383.5 4.6 collective-permute-start.13
  436.6 11.1 %collective-permute-start.14 = (f32[512,256]{1,0:T(8,128)S(1)}, f32[512,256]{1,0:T(8,128)S(1)}, u32[]{:S(2)}, u32[]{:S(2)}) collective-permute-start(f32[512,256]{1,0:T(8,128)S(1)} %get-tuple-element.112), channel_id=1, source_target_pairs={{2,8},{3,9},{4,10},{5,11},{6,12},{7,13},{8,0},{9,1},{10,2},{11,3},... | collective-permute-start | bytes 1572872 | tf_op jit(solution)/shard_map/ppermute | solution.py:63
  438.1 9.6 %copy-start.6 = (f32[2048,256]{1,0:T(8,128)S(1)}, f32[2048,256]{1,0:T(8,128)}, u32[]{:S(2)}) copy-start(f32[2048,256]{1,0:T(8,128)} %get-tuple-element.156) | copy-start | bytes 6291460
  438.1 9.6 %copy-start.35 = (f32[1,256]{1,0:T(1,128)S(1)}, f32[1,256]{1,0:T(1,128)}, u32[]{:S(2)}) copy-start(f32[1,256]{1,0:T(1,128)} %copy-done.34) | copy-start | bytes 3076
  438.1 9.6 %collective-permute-start.15 = (f32[512,256]{1,0:T(8,128)S(1)}, f32[512,256]{1,0:T(8,128)S(1)}, u32[]{:S(2)}, u32[]{:S(2)}) collective-permute-start(f32[512,256]{1,0:T(8,128)S(1)} %get-tuple-element.113), channel_id=1, source_target_pairs={{0,8},{1,9},{2,10},{3,11},{4,12},{5,13},{6,14},{7,15},{8,2},{9,3},... | collective-permute-start | bytes 1572872 | tf_op jit(solution)/shard_map/ppermute | solution.py:63
  447.7 11.4 %copy-start.47 = (f32[1,1,256]{2,1,0:T(1,128)S(1)}, f32[1,1,256]{2,1,0:T(1,128)}, u32[]{:S(2)}) copy-start(f32[1,1,256]{2,1,0:T(1,128)} %copy-done.46) | copy-start | bytes 3076
  447.7 12.1 %copy-start.7 = (f32[2048,256]{1,0:T(8,128)S(1)}, f32[2048,256]{1,0:T(8,128)}, u32[]{:S(2)}) copy-start(f32[2048,256]{1,0:T(8,128)} %get-tuple-element.156) | copy-start | bytes 6291460
  465.5 41.0 %copy-start = (f32[2048,512]{1,0:T(8,128)}, f32[2048,512]{1,0:T(8,128)S(1)}, u32[]{:S(2)}) copy-start(f32[2048,512]{1,0:T(8,128)S(1)} %fusion.70) | copy-start | bytes 12582916
  490.9 15.6 %collective-permute-start.16 = (f32[512,256]{1,0:T(8,128)S(1)}, f32[512,256]{1,0:T(8,128)S(1)}, u32[]{:S(2)}, u32[]{:S(2)}) collective-permute-start(f32[512,256]{1,0:T(8,128)S(1)} %get-tuple-element.110), channel_id=1, source_target_pairs={{2,8},{3,9},{4,10},{5,11},{6,12},{7,13},{8,0},{9,1},{10,2},{11,3},... | collective-permute-start | bytes 1572872 | tf_op jit(solution)/shard_map/ppermute | solution.py:63
  492.4 9.3 %copy-start.3 = (f32[2048,256]{1,0:T(8,128)S(1)}, f32[2048,256]{1,0:T(8,128)}, u32[]{:S(2)}) copy-start(f32[2048,256]{1,0:T(8,128)} %copy-done.2) | copy-start | bytes 6291460
  492.4 9.3 %copy-start.13 = (f32[2048,256]{1,0:T(8,128)S(1)}, f32[2048,256]{1,0:T(8,128)}, u32[]{:S(2)}) copy-start(f32[2048,256]{1,0:T(8,128)} %copy-done.12) | copy-start | bytes 6291460
  492.4 9.3 %copy-start.15 = (f32[2048,256]{1,0:T(8,128)S(1)}, f32[2048,256]{1,0:T(8,128)}, u32[]{:S(2)}) copy-start(f32[2048,256]{1,0:T(8,128)} %fusion.8) | copy-start | bytes 6291460
  492.4 14.1 %collective-permute-start.17 = (f32[512,256]{1,0:T(8,128)S(1)}, f32[512,256]{1,0:T(8,128)S(1)}, u32[]{:S(2)}, u32[]{:S(2)}) collective-permute-start(f32[512,256]{1,0:T(8,128)S(1)} %get-tuple-element.111), channel_id=1, source_target_pairs={{0,8},{1,9},{2,10},{3,11},{4,12},{5,13},{6,14},{7,15},{8,2},{9,3},... | collective-permute-start | bytes 1572872 | tf_op jit(solution)/shard_map/ppermute | solution.py:63
  509.8 7.0 %copy-start.31 = (f32[100,64]{0,1:T(8,128)S(1)}, f32[100,64]{0,1:T(8,128)}, u32[]{:S(2)}) copy-start(f32[100,64]{0,1:T(8,128)} %param.35) | copy-start | bytes 76804
  509.8 16.2 %copy-start.55 = (f32[1,1,256]{2,1,0:T(1,128)S(1)}, f32[1,1,256]{2,1,0:T(1,128)}, u32[]{:S(2)}) copy-start(f32[1,1,256]{2,1,0:T(1,128)} %copy-done.54) | copy-start | bytes 3076
  509.8 154.1 %all-gather.7.cloned.1.call-start = ((), (), s32[]{:S(2)}) async-start(), calls=%async_computation.1 | async-start | bytes 1966080 | tf_op jit(solution)/shard_map/all_gather | solution.py:328
  529.0 44.9 %copy-start.60 = (f32[47]{0:T(128)S(1)}, f32[47]{0:T(128)}, u32[]{:S(2)}) copy-start(f32[47]{0:T(128)} %param.34) | copy-start | bytes 568
  529.0 44.9 %copy-start.61 = (f32[47]{0:T(128)S(1)}, f32[47]{0:T(128)}, u32[]{:S(2)}) copy-start(f32[47]{0:T(128)} %param.43) | copy-start | bytes 568
  529.0 44.9 %copy-start.62 = (f32[47]{0:T(128)S(1)}, f32[47]{0:T(128)}, u32[]{:S(2)}) copy-start(f32[47]{0:T(128)} %param.40) | copy-start | bytes 568
  529.1 45.4 %copy-start.51 = (f32[4,256]{1,0:T(4,128)S(1)}, f32[4,256]{1,0:T(4,128)}, u32[]{:S(2)}) copy-start(f32[4,256]{1,0:T(4,128)} %param.32) | copy-start | bytes 12292
  529.1 45.4 %copy-start.56 = (f32[4,256]{1,0:T(4,128)S(1)}, f32[4,256]{1,0:T(4,128)}, u32[]{:S(2)}) copy-start(f32[4,256]{1,0:T(4,128)} %param.41) | copy-start | bytes 12292
  529.1 45.4 %copy-start.57 = (f32[4,256]{1,0:T(4,128)S(1)}, f32[4,256]{1,0:T(4,128)}, u32[]{:S(2)}) copy-start(f32[4,256]{1,0:T(4,128)} %param.38) | copy-start | bytes 12292
  529.1 46.0 %copy-start.32 = (f32[3,2,256]{2,1,0:T(2,128)S(1)}, f32[3,2,256]{2,1,0:T(2,128)}, u32[]{:S(2)}) copy-start(f32[3,2,256]{2,1,0:T(2,128)} %param.33) | copy-start | bytes 18436
  529.1 46.0 %copy-start.52 = (f32[3,2,256]{2,1,0:T(2,128)S(1)}, f32[3,2,256]{2,1,0:T(2,128)}, u32[]{:S(2)}) copy-start(f32[3,2,256]{2,1,0:T(2,128)} %param.42) | copy-start | bytes 18436
  529.1 46.0 %copy-start.53 = (f32[3,2,256]{2,1,0:T(2,128)S(1)}, f32[3,2,256]{2,1,0:T(2,128)}, u32[]{:S(2)}) copy-start(f32[3,2,256]{2,1,0:T(2,128)} %param.39) | copy-start | bytes 18436
  573.9 111.9 %copy-start.27 = (f32[64,47]{0,1:T(8,128)}, f32[64,47]{0,1:T(8,128)S(1)}, u32[]{:S(2)}) copy-start(f32[64,47]{0,1:T(8,128)S(1)} %constant_dynamic-slice_fusion) | copy-start | bytes 36100
  666.0 18.9 %copy-start.26 = (f32[100,64]{0,1:T(8,128)S(1)}, f32[100,64]{0,1:T(8,128)}, u32[]{:S(2)}) copy-start(f32[100,64]{0,1:T(8,128)} %param.29) | copy-start | bytes 76804
  666.0 19.8 %copy-start.29 = (f32[64,47]{0,1:T(8,128)S(1)}, f32[64,47]{0,1:T(8,128)}, u32[]{:S(2)}) copy-start(f32[64,47]{0,1:T(8,128)} %param.31) | copy-start | bytes 36100
  666.0 20.6 %copy-start.23 = (f32[3,128,256]{2,1,0:T(8,128)S(1)}, f32[3,128,256]{2,1,0:T(8,128)}, u32[]{:S(2)}) copy-start(f32[3,128,256]{2,1,0:T(8,128)} %param.30) | copy-start | bytes 1179652
  666.1 22.0 %copy-start.24 = (f32[3,128,256]{2,1,0:T(8,128)}, f32[3,128,256]{2,1,0:T(8,128)S(1)}, u32[]{:S(2)}) copy-start(f32[3,128,256]{2,1,0:T(8,128)S(1)} %constant_dynamic-slice_fusion.1) | copy-start | bytes 1179652
  (22 other events, 71.7 us)
Sparse Core Ops, SparseCore 0:
  9.6 23.0 all-gather.4
  509.9 133.5 all-reduce.11
  645.2 18.6 all-gather.6

commit v2 on v1

--- a/solution.py
+++ b/solution.py
@@ -9,8 +9,12 @@
 from jax.sharding import PartitionSpec as P
 
 NS_STEPS = 5
+FORWARD_PARTS = (2, 2, 2)
 
 f32 = jnp.float32
+bf16 = jnp.bfloat16
+LANES = 128
+TILE = 256
 highest = lax.Precision.HIGHEST
 three_pass = lax.Precision.HIGH
 norm_epsilon = 1e-05
@@ -238,45 +242,543 @@
     )(conv_mom, in_pad, head_t)
 
 
-def layer_forward(hidden, matrix, bias, gain, shift, adjacency, rim_below, rim_above, node_count, dims):
-    halo_rows = rim_below.shape[0]
-    rows_dev = hidden.shape[0]
-    below = pass_rows(hidden[rows_dev - halo_rows :], *dims, 1)
-    above = pass_rows(hidden[:halo_rows], *dims, -1)
-    padded = jnp.concatenate([below * rim_below, hidden, above * rim_above], 0)
-    joined = jnp.concatenate([hidden, product(adjacency, padded)], 1)
-    pre = product(joined, matrix) + bias
-    active = jnp.maximum(pre, 0.0)
-    totals = group_sum(jnp.stack([jnp.sum(active, 0), jnp.sum(active * active, 0)]), dims[1])
-    mean = totals[0] / node_count
-    inverse = lax.rsqrt(totals[1] / node_count - mean * mean + norm_epsilon)
-    normed = (active - mean) * inverse
-    return (gain * normed + shift, (joined, pre, normed, inverse))
-
-
-def layer_backward(grad_out, kept, matrix, gain, adjacency, rim_below, rim_above, node_count, dims):
-    joined, pre, normed, inverse = kept
-    halo_rows = rim_below.shape[0]
-    rows_dev = joined.shape[0]
-    width = matrix.shape[1]
-    grad_gain = jnp.sum(grad_out * normed, 0)
-    grad_shift = jnp.sum(grad_out, 0)
-    totals = group_sum(jnp.stack([grad_shift, grad_gain]), dims[1]) * gain
-    grad_normed = grad_out * gain
-    grad_active = inverse * (
-        grad_normed - totals[0] / node_count - normed * (totals[1] / node_count)
+def order_kernel(wide, to_ref, from_ref, w_ref, key_out, w_out, col_out, lo_out, hi_out):
+    to, frm = to_ref[...], from_ref[...]
+    key = (((to >> 8) * wide + (frm >> 8)) << 16) | ((to & 255) << 8) | (frm & 255)
+    shape3 = (16, 8, LANES)
+    key = key.astype(f32).reshape(shape3)
+    w = w_ref[...].reshape(shape3)
+    sub = lax.broadcasted_iota(jnp.int32, shape3, 1)
+    lane = lax.broadcasted_iota(jnp.int32, shape3, 2)
+    vreg = lax.broadcasted_iota(jnp.int32, shape3, 0)
+    place = vreg + 16 * sub + 128 * lane
+    for phase in range(14):
+        for bit in range(phase, -1, -1):
+            down = ((place >> (phase + 1)) & 1) == 1
+            if bit < 4:
+                view = (16 >> (bit + 1), 2, 1 << bit, 8, LANES)
+                kv, wv = key.reshape(view), w.reshape(view)
+                dv = down.astype(jnp.int32).reshape(view)[:, 0] == 1
+                a, b, wa, wb = kv[:, 0], kv[:, 1], wv[:, 0], wv[:, 1]
+                turn = jnp.logical_xor(a > b, dv)
+                key = jnp.stack([jnp.where(turn, b, a), jnp.where(turn, a, b)], 1).reshape(shape3)
+                w = jnp.stack([jnp.where(turn, wb, wa), jnp.where(turn, wa, wb)], 1).reshape(shape3)
+            else:
+                if bit < 7:
+                    axis, gap, size, pos = 1, 1 << (bit - 4), 8, sub
+                else:
+                    axis, gap, size, pos = 2, 1 << (bit - 7), LANES, lane
+                low = (pos & gap) == 0
+                kp = jnp.where(low, pltpu.roll(key, size - gap, axis), pltpu.roll(key, gap, axis))
+                wp = jnp.where(low, pltpu.roll(w, size - gap, axis), pltpu.roll(w, gap, axis))
+                smaller = jnp.logical_xor(low, down)
+                take = jnp.where(smaller, kp, key) < jnp.where(smaller, key, kp)
+                key = jnp.where(take, kp, key)
+                w = jnp.where(take, wp, w)
+    flat = key.reshape(LANES, LANES)
+    key_out[...] = flat.T.astype(jnp.int32)
+    w_out[...] = w.reshape(LANES, LANES).T
+    start = (lax.broadcasted_iota(jnp.int32, (8, LANES), 1).astype(f32) * 65536.0)[None]
+    below = jnp.zeros(shape3, f32)
+    upto = jnp.zeros(shape3, f32)
+    for c in range(LANES):
+        wide_key = jnp.broadcast_to(flat[:, c : c + 1], (LANES, LANES))
+        col_out[c] = (wide_key - jnp.floor(wide_key * (1.0 / 256.0)) * 256.0).astype(bf16)
+        wide_key = wide_key.reshape(shape3)
+        below = below + jnp.where(wide_key < start, 1.0, 0.0)
+        upto = upto + jnp.where(wide_key < start + 65536.0, 1.0, 0.0)
+    n_below = jnp.sum(below.reshape(LANES, LANES), axis=0, keepdims=True)
+    n_upto = jnp.sum(upto.reshape(LANES, LANES), axis=0, keepdims=True)
+    first = jnp.floor(n_below * (1.0 / 128.0))
+    end = jnp.floor((n_upto + 127.0) * (1.0 / 128.0))
+    lo_out[...] = first.astype(jnp.int32)
+    hi_out[...] = jnp.where(n_upto > n_below, end, first).astype(jnp.int32)
+
+
+def order_edges(to, frm, w, wide):
+    vmem = pl.BlockSpec(memory_space=pltpu.VMEM)
+    return pl.pallas_call(
+        functools.partial(order_kernel, wide),
+        out_shape=(
+            jax.ShapeDtypeStruct((LANES, LANES), jnp.int32),
+            jax.ShapeDtypeStruct((LANES, LANES), f32),
+            jax.ShapeDtypeStruct((LANES, LANES, LANES), bf16),
+            jax.ShapeDtypeStruct((1, LANES), jnp.int32),
+            jax.ShapeDtypeStruct((1, LANES), jnp.int32),
+        ),
+        in_specs=[vmem] * 3,
+        out_specs=(vmem,) * 5,
+        compiler_params=pltpu.CompilerParams(vmem_limit_bytes=40 << 20),
+        name="order_edges",
+    )(to.reshape(LANES, LANES), frm.reshape(LANES, LANES), w.reshape(LANES, LANES))
+
+
+def fill_kernel(wide, rim, chunk, parts, lo, hi, rims, key_ref, w_ref, col_ref, *refs):
+    outs, sums, acc, rowacc = refs[:parts], refs[parts], refs[parts + 1], refs[parts + 2]
+    i = pl.program_id(0)
+    pack = 16
+    shape = (TILE // pack, pack, LANES)
+    rows = lax.broadcasted_iota(jnp.int32, shape, 0) * pack + lax.broadcasted_iota(jnp.int32, shape, 1)
+    rows = rows.astype(f32).astype(bf16)
+    lanes = lax.broadcasted_iota(jnp.int32, (LANES, LANES), 1).astype(f32)
+    lanes0, lanes1 = lanes.astype(bf16), (lanes + 128.0).astype(bf16)
+    one, zero = jnp.ones((), bf16), jnp.zeros((), bf16)
+
+    def spread(row):
+        return jnp.broadcast_to(row, (pack, LANES)).astype(bf16)[None]
+
+    rowacc[...] = jnp.zeros_like(rowacc)
+
+    def tile(j, _):
+        b = i * wide + j
+        first, end = lo[0, b], hi[0, b]
+        end = jnp.where(jnp.logical_and(j < rim, rims[0] == 0), first, end)
+        end = jnp.where(jnp.logical_and(j >= wide - rim, rims[1] == 0), first, end)
+        cols = pl.ds(pl.multiple_of(j * TILE, TILE), TILE)
+
+        @pl.when(end <= first)
+        def _():
+            for out in outs:
+                out[:, cols] = jnp.zeros((TILE, TILE), bf16)
+
+        @pl.when(end > first)
+        def _():
+            def part(base, c):
+                row = jnp.minimum(base + c, LANES - 1)
+                here = key_ref[pl.ds(row, 1), :] - (b << 16)
+                if c:
+                    here = jnp.where(base + c < end, here, -1)
+                at = rows == spread((here >> 8).astype(f32))
+                rest = w_ref[pl.ds(row, 1), :]
+                left = []
+                for q in range(parts):
+                    piece = rest.astype(bf16).astype(f32)
+                    rest = rest - piece
+                    left.append(jnp.where(at, spread(piece), zero).reshape(TILE, LANES))
+                col = col_ref[row]
+                right = jnp.concatenate(
+                    [jnp.where(col == lanes0, one, zero), jnp.where(col == lanes1, one, zero)], 1
+                )
+                return left, right
+
+            def get(base):
+                made = [part(base, c) for c in range(chunk)]
+                lhs = jnp.concatenate([m[0][q] for q in range(parts) for m in made], 1)
+                rhs = jnp.concatenate([m[1] for m in made] * parts, 0)
+                return jnp.dot(lhs, rhs, preferred_element_type=f32)
+
+            acc[...] = get(first)
+
+            def more(t, _):
+                acc[...] += get(first + t * chunk)
+                return 0
+
+            lax.fori_loop(1, lax.div(end - first + chunk - 1, chunk), more, 0)
+            rest = acc[...]
+            rowacc[...] += rest[:, :LANES] + rest[:, LANES:]
+            for out in outs:
+                piece = rest.astype(bf16)
+                out[:, cols] = piece
+                rest = rest - piece.astype(f32)
+
+        return 0
+
+    lax.fori_loop(0, wide, tile, 0)
+    sums[...] = jnp.broadcast_to(jnp.sum(rowacc[...], axis=1, keepdims=True), sums.shape)
+
+
+def fill(order, rims, tiles, wide, rim, parts, chunk=4):
+    key, w, col, lo, hi = order
+    cols = wide * TILE
+    return pl.pallas_call(
+        functools.partial(fill_kernel, wide, rim, chunk, parts),
+        out_shape=tuple(jax.ShapeDtypeStruct((tiles * TILE, cols), bf16) for _ in range(parts))
+        + (jax.ShapeDtypeStruct((tiles * TILE, LANES), f32),),
+        grid_spec=pltpu.PrefetchScalarGridSpec(
+            num_scalar_prefetch=3,
+            grid=(tiles,),
+            in_specs=[pl.BlockSpec((LANES, LANES), lambda i, *_: (0, 0))] * 2
+            + [pl.BlockSpec((LANES, LANES, LANES), lambda i, *_: (0, 0, 0))],
+            out_specs=tuple(pl.BlockSpec((TILE, cols), lambda i, *_: (i, 0)) for _ in range(parts))
+            + (pl.BlockSpec((TILE, LANES), lambda i, *_: (i, 0)),),
+            scratch_shapes=[pltpu.VMEM((TILE, TILE), f32), pltpu.VMEM((TILE, LANES), f32)],
+        ),
+        compiler_params=pltpu.CompilerParams(vmem_limit_bytes=50 << 20),
+        name="fill_tiles",
+    )(lo, hi, rims, key, w, col)
+
+
+def parts_of(x, count):
+    found = []
+    for q in range(count):
+        piece = x.astype(bf16)
+        found.append(piece)
+        if q + 1 < count:
+            x = x - piece.astype(f32)
+    return found
+
+
+def pair_list(count):
+    return [(p, q) for p in range(count) for q in range(count) if p + q < count]
+
+
+def dots(left, right, dims=((1,), (0,))):
+    total = None
+    for p, q in pair_list(len(left)):
+        piece = lax.dot_general(left[p], right[q], (dims, ((), ())), preferred_element_type=f32)
+        total = piece if total is None else total + piece
+    return total
+
+
+def start_stats(n, batch, block, src, held, send_sem, recv_sem):
+    copies = []
+    for k in range(1, n):
+        copy = pltpu.make_async_remote_copy(
+            src_ref=src,
+            dst_ref=held.at[k],
+            send_sem=send_sem.at[k],
+            recv_sem=recv_sem.at[k],
+            device_id=peer_place(batch, lax.rem(block + k, n)),
+            device_id_type=pl.DeviceIdType.MESH,
+        )
+        copy.start()
+        copies.append(copy)
+    held[0] = src[...]
+    return copies
+
+
+def finish_stats(n, block, copies, held):
+    for copy in copies:
+        copy.wait()
+    total = held[lax.rem(block, n)]
+    for q in range(1, n):
+        total = total + held[lax.rem(block + n - q, n)]
+    return total
+
+
+def rim_copy(batch, to, src, dst, sems, which):
+    return pltpu.make_async_remote_copy(
+        src_ref=src,
+        dst_ref=dst,
+        send_sem=sems[0].at[which],
+        recv_sem=sems[1].at[which],
+        device_id=peer_place(batch, to),
+        device_id_type=pl.DeviceIdType.MESH,
     )
-    grad_pre = jnp.where(pre > 0.0, grad_active, 0.0)
-    grad_matrix = product3(joined.T, grad_pre)
-    grad_bias = jnp.sum(grad_pre, 0)
-    grad_joined = product3(grad_pre, matrix.T)
-    grad_padded = product3(adjacency.T, grad_joined[:, width:])
-    from_above = pass_rows(grad_padded[:halo_rows] * rim_below, *dims, -1)
-    from_below = pass_rows(grad_padded[halo_rows + rows_dev :] * rim_above, *dims, 1)
-    grad_hidden = grad_joined[:, :width] + grad_padded[halo_rows : halo_rows + rows_dev]
-    grad_hidden = grad_hidden + jnp.pad(from_above, ((rows_dev - halo_rows, 0), (0, 0)))
-    grad_hidden = grad_hidden + jnp.pad(from_below, ((0, rows_dev - halo_rows), (0, 0)))
-    return (grad_hidden, grad_matrix, grad_bias, grad_gain, grad_shift)
+
+
+def load_adjacency(hbm, vmem, sem, height):
+    copies = []
+    steps = vmem[0].shape[0] // height
+    for s in range(steps):
+        here = pl.ds(s * height, height)
+        copies.append(
+            [
+                pltpu.make_async_copy(src.at[here], dst.at[here], sem.at[s * len(hbm) + q])
+                for q, (src, dst) in enumerate(zip(hbm, vmem))
+            ]
+        )
+    for group in copies[:2]:
+        for copy in group:
+            copy.start()
+    return copies
+
+
+def next_rows(copies, s):
+    for copy in copies[s]:
+        copy.wait()
+    if s + 2 < len(copies):
+        for copy in copies[s + 2]:
+            copy.start()
+
+
+def column_sums(x):
+    return jnp.sum(x, axis=0, keepdims=True)
+
+
+def forward_kernel(n, normed, parts, nodes, height, x_ref, stat_ref, param_ref, w_ref, bias_ref, sums_ref, *refs):
+    a_hbm, refs = refs[:parts], refs[parts:]
+    out_ref, agg_ref, stat_out, affine_out = refs[:4]
+    refs = refs[4:]
+    a, refs = refs[:parts], refs[parts:]
+    xs, refs = refs[:parts], refs[parts:]
+    rim, held, a_sem, send_sem, recv_sem, rim_send, rim_recv = refs
+    batch, block = my_place()
+    rows, width = x_ref.shape
+    halo = rim.shape[1]
+    greet(n, batch, block)
+    sems = (rim_send, rim_recv)
+    up = rim_copy(batch, lax.rem(block + 1, n), x_ref.at[pl.ds(rows - halo, halo)], rim.at[0], sems, 0)
+    down = rim_copy(batch, lax.rem(block + n - 1, n), x_ref.at[pl.ds(0, halo)], rim.at[1], sems, 1)
+    first, last = block == 0, block == n - 1
+
+    @pl.when(jnp.logical_not(last))
+    def _():
+        up.start()
+
+    @pl.when(jnp.logical_not(first))
+    def _():
+        down.start()
+
+    if normed:
+        copies = start_stats(n, batch, block, stat_ref, held, send_sem, recv_sem)
+    loads = load_adjacency(a_hbm, a, a_sem, height)
+
+    @pl.when(first)
+    def _():
+        rim[0] = jnp.zeros((halo, width), f32)
+
+    @pl.when(last)
+    def _():
+        rim[1] = jnp.zeros((halo, width), f32)
+
+    step = 256
+    for s in range(rows // step):
+        here = pl.ds(s * step, step)
+        for dst, piece in zip(xs, parts_of(x_ref[here, :], parts)):
+            dst[pl.ds(halo + s * step, step), :] = piece
+    own = pl.ds(halo, rows)
+    for s in range(len(loads)):
+        next_rows(loads, s)
+        here = pl.ds(s * height, height)
+        agg_ref[here, :] = dots([q[here, own] for q in a], [q[own, :] for q in xs])
+    if normed:
+        totals = finish_stats(n, block, copies, held) * (1.0 / nodes)
+        mean = totals[0:1]
+        inverse = lax.rsqrt(totals[1:2] - mean * mean + norm_epsilon)
+        scale = param_ref[0:1] * inverse
+        offset = param_ref[1:2] - mean * scale
+        affine_out[0:1] = mean
+        affine_out[1:2] = inverse
+        affine_out[2:3] = scale
+        affine_out[3:4] = offset
+    else:
+        affine_out[...] = jnp.zeros_like(affine_out)
+
+    @pl.when(jnp.logical_not(first))
+    def _():
+        rim_copy(batch, block, rim.at[0], rim.at[0], sems, 0).wait_recv()
+
+    @pl.when(jnp.logical_not(last))
+    def _():
+        rim_copy(batch, block, rim.at[1], rim.at[1], sems, 1).wait_recv()
+
+    for dst, low, high in zip(xs, parts_of(rim[0], parts), parts_of(rim[1], parts)):
+        dst[pl.ds(0, halo), :] = low
+        dst[pl.ds(halo + rows, halo), :] = high
+    stat_out[...] = jnp.zeros_like(stat_out)
+    weights = parts_of(w_ref[...], 3)
+    lower, upper = pl.ds(0, halo), pl.ds(halo + rows, halo)
+
+    def finish(s, _):
+        here = pl.ds(pl.multiple_of(s * step, step), step)
+        agg = agg_ref[here, :]
+        agg = agg + dots([q[here, lower] for q in a], [q[lower, :] for q in xs])
+        agg = agg + dots([q[here, upper] for q in a], [q[upper, :] for q in xs])
+        h = x_ref[here, :]
+        if normed:
+            row_sum = sums_ref[here, :]
+            agg = agg * scale + jnp.concatenate([row_sum, row_sum], 1) * offset
+            h = h * scale + offset
+        agg_ref[here, :] = agg
+        joined = jnp.concatenate([h, agg], 1)
+        pre = dots(parts_of(joined, 3), weights) + bias_ref[...]
+        active = jnp.maximum(pre, 0.0)
+        out_ref[here, :] = active
+        stat_out[0:1] += column_sums(active)
+        stat_out[1:2] += column_sums(active * active)
+        return 0
+
+    lax.fori_loop(0, rows // step, finish, 0)
+
+    @pl.when(jnp.logical_not(last))
+    def _():
+        up.wait_send()
+
+    @pl.when(jnp.logical_not(first))
+    def _():
+        down.wait_send()
+
+
+def forward_layer(n, normed, nodes, x, stats, params, w_parts, bias, sums, a, collective_id):
+    rows, width = x.shape
+    parts = len(a)
+    cols = a[0].shape[1]
+    halo = (cols - rows) // 2
+    height = 256
+    vmem = pl.BlockSpec(memory_space=pltpu.VMEM)
+    steps = rows // height
+    return pl.pallas_call(
+        functools.partial(forward_kernel, n, normed, parts, nodes, height),
+        out_shape=(
+            jax.ShapeDtypeStruct((rows, width), f32),
+            jax.ShapeDtypeStruct((rows, width), f32),
+            jax.ShapeDtypeStruct((2, width), f32),
+            jax.ShapeDtypeStruct((4, width), f32),
+        ),
+        in_specs=[vmem] * 6 + [pl.BlockSpec(memory_space=pl.ANY)] * parts,
+        out_specs=(vmem,) * 4,
+        scratch_shapes=[pltpu.VMEM((rows, cols), bf16) for _ in range(parts)]
+        + [pltpu.VMEM((cols, width), bf16) for _ in range(parts)]
+        + [
+            pltpu.VMEM((2, halo, width), f32),
+            pltpu.VMEM((n, 2, width), f32),
+            pltpu.SemaphoreType.DMA((steps * parts,)),
+            pltpu.SemaphoreType.DMA((n,)),
+            pltpu.SemaphoreType.DMA((n,)),
+            pltpu.SemaphoreType.DMA((2,)),
+            pltpu.SemaphoreType.DMA((2,)),
+        ],
+        compiler_params=pltpu.CompilerParams(
+            collective_id=collective_id, has_side_effects=True, vmem_limit_bytes=62 << 20
+        ),
+        name="forward_layer",
+    )(x, stats, params, w_parts, bias, sums, *a)
+
+
+def backward_kernel(n, below_normed, nodes, height, g_ref, stat_ref, affine_ref, gain_ref, act_ref, agg_ref, x_ref,
+                    below_ref, wt_ref, a1_hbm, a2_hbm, out_ref, gw_ref, gb_ref, stat_out, a1, a2, g1, g2, b1, b2,
+                    out_rim, rim, held, a_sem, send_sem, recv_sem, rim_send, rim_recv):
+    batch, block = my_place()
+    rows, width = g_ref.shape
+    halo = rim.shape[1]
+    a = (a1, a2)
+    greet(n, batch, block)
+    copies = start_stats(n, batch, block, stat_ref, held, send_sem, recv_sem)
+    loads = load_adjacency((a1_hbm, a2_hbm), a, a_sem, height)
+    first, last = block == 0, block == n - 1
+    sems = (rim_send, rim_recv)
+    mean, inverse = affine_ref[0:1], affine_ref[1:2]
+    gain = gain_ref[...]
+    totals = finish_stats(n, block, copies, held) * gain * (1.0 / nodes)
+    gb_ref[...] = jnp.zeros_like(gb_ref)
+    w_t = parts_of(wt_ref[...], 2)
+    step = 256
+
+    def enter(s, _):
+        here = pl.ds(pl.multiple_of(s * step, step), step)
+        act = act_ref[here, :]
+        normed = (act - mean) * inverse
+        grad = inverse * (g_ref[here, :] * gain - totals[0:1] - normed * totals[1:2])
+        grad = jnp.where(act > 0.0, grad, 0.0)
+        gb_ref[...] += column_sums(grad)
+        pieces = parts_of(grad, 2)
+        g1[here, :] = pieces[0]
+        g2[here, :] = pieces[1]
+        joined = dots(pieces, w_t)
+        out_ref[here, :] = joined[:, :width]
+        pieces = parts_of(joined[:, width:], 2)
+        b1[here, :] = pieces[0]
+        b2[here, :] = pieces[1]
+        return 0
+
+    lax.fori_loop(0, rows // step, enter, 0)
+    for s in range(len(loads)):
+        next_rows(loads, s)
+    turned = ((0,), (0,))
+    b = [b1[...], b2[...]]
+    out_rim[0] = dots([q[:, pl.ds(0, halo)] for q in a], b, turned)
+    down = rim_copy(batch, lax.rem(block + n - 1, n), out_rim.at[0], rim.at[0], sems, 0)
+    up = rim_copy(batch, lax.rem(block + 1, n), out_rim.at[1], rim.at[1], sems, 1)
+
+    @pl.when(jnp.logical_not(first))
+    def _():
+        down.start()
+
+    out_rim[1] = dots([q[:, pl.ds(halo + rows, halo)] for q in a], b, turned)
+
+    @pl.when(jnp.logical_not(last))
+    def _():
+        up.start()
+
+    wide = 512
+
+    def own(s, _):
+        here = pl.ds(pl.multiple_of(s * wide, wide), wide)
+        cols = pl.ds(pl.multiple_of(halo + s * wide, 128), wide)
+        out_ref[here, :] += dots([q[:, cols] for q in a], b, turned)
+        return 0
+
+    lax.fori_loop(0, rows // wide, own, 0)
+    gw_ref[...] = jnp.zeros_like(gw_ref)
+
+    def weights(s, _):
+        here = pl.ds(pl.multiple_of(s * wide, wide), wide)
+        h = x_ref[here, :]
+        if below_normed:
+            h = h * below_ref[2:3] + below_ref[3:4]
+        g = [g1[here, :], g2[here, :]]
+        gw_ref[pl.ds(0, width), :] += dots(parts_of(h, 2), g, turned)
+        gw_ref[pl.ds(width, width), :] += dots(parts_of(agg_ref[here, :], 2), g, turned)
+        return 0
+
+    lax.fori_loop(0, rows // wide, weights, 0)
+
+    @pl.when(jnp.logical_not(last))
+    def _():
+        rim_copy(batch, block, rim.at[0], rim.at[0], sems, 0).wait_recv()
+        out_ref[pl.ds(rows - halo, halo), :] += rim[0]
+
+    @pl.when(jnp.logical_not(first))
+    def _():
+        rim_copy(batch, block, rim.at[1], rim.at[1], sems, 1).wait_recv()
+        out_ref[pl.ds(0, halo), :] += rim[1]
+
+    stat_out[...] = jnp.zeros_like(stat_out)
+
+    def tail(s, _):
+        here = pl.ds(pl.multiple_of(s * step, step), step)
+        grad = out_ref[here, :]
+        stat_out[0:1] += column_sums(grad)
+        if below_normed:
+            stat_out[1:2] += column_sums(grad * ((x_ref[here, :] - below_ref[0:1]) * below_ref[1:2]))
+        return 0
+
+    lax.fori_loop(0, rows // step, tail, 0)
+
+    @pl.when(jnp.logical_not(first))
+    def _():
+        down.wait_send()
+
+    @pl.when(jnp.logical_not(last))
+    def _():
+        up.wait_send()
+
+
+def backward_layer(n, below_normed, nodes, g, stats, affine, gain, act, agg, x, below, w_t, a, collective_id):
+    rows, width = x.shape
+    cols = a[0].shape[1]
+    halo = (cols - rows) // 2
+    height = 512
+    vmem = pl.BlockSpec(memory_space=pltpu.VMEM)
+    steps = rows // height
+    return pl.pallas_call(
+        functools.partial(backward_kernel, n, below_normed, nodes, height),
+        out_shape=(
+            jax.ShapeDtypeStruct((rows, width), f32),
+            jax.ShapeDtypeStruct((2 * width, width), f32),
+            jax.ShapeDtypeStruct((1, width), f32),
+            jax.ShapeDtypeStruct((2, width), f32),
+        ),
+        in_specs=[vmem] * 9 + [pl.BlockSpec(memory_space=pl.ANY)] * 2,
+        out_specs=(vmem,) * 4,
+        scratch_shapes=[pltpu.VMEM((rows, cols), bf16)] * 2
+        + [pltpu.VMEM((rows, width), bf16)] * 4
+        + [
+            pltpu.VMEM((2, halo, width), f32),
+            pltpu.VMEM((2, halo, width), f32),
+            pltpu.VMEM((n, 2, width), f32),
+            pltpu.SemaphoreType.DMA((steps * 2,)),
+            pltpu.SemaphoreType.DMA((n,)),
+            pltpu.SemaphoreType.DMA((n,)),
+            pltpu.SemaphoreType.DMA((2,)),
+            pltpu.SemaphoreType.DMA((2,)),
+        ],
+        compiler_params=pltpu.CompilerParams(
+            collective_id=collective_id, has_side_effects=True, vmem_limit_bytes=62 << 20
+        ),
+        name="backward_layer",
+    )(g, stats, affine, gain, act, agg, x, below, w_t, *a)
 
 
 def adamw(param, grad, first, second, count):
@@ -335,31 +837,39 @@
     node_count = rows_dev * n_rows
     all_nodes = node_count * n_batch
     edges = edge_rows[0, 0]
-    counts = halo_counts[0, 0]
-    adjacency = (
-        jnp.zeros((rows_dev, rows_dev + 2 * halo_rows), f32)
-        .at[edges[0], edges[1]]
-        .add(edge_weight[0, 0])
-    )
-    place = jnp.arange(halo_rows, dtype=jnp.int32)
-    rim_below = (place >= halo_rows - counts[0]).astype(f32)[:, None]
-    rim_above = (place < counts[1]).astype(f32)[:, None]
-    hidden = product(inputs, full_in) + biases[0]
-    kept_all = []
+    block = my_place()[1]
+    wide = (rows_dev + 2 * halo_rows) // TILE
+    rims = jnp.stack([(block > 0).astype(jnp.int32), (block < n_rows - 1).astype(jnp.int32)])
+    order = order_edges(edges[0], edges[1], edge_weight[0, 0], wide)
+    *adjacency, row_sums = fill(order, rims, rows_dev // TILE, wide, halo_rows // TILE, 3)
+    w_turned = jnp.swapaxes(full_conv, 1, 2)
+    x = product(inputs, full_in) + biases[0]
+    xs, aggs, affines = [x], [], []
+    stats = jnp.zeros((2, x.shape[1]), f32)
     for layer in range(layers):
-        hidden, kept = layer_forward(
-            hidden,
+        used = FORWARD_PARTS[min(layer, len(FORWARD_PARTS) - 1)]
+        x, agg, stats, affine = forward_layer(
+            n_rows,
+            layer > 0,
+            node_count,
+            x,
+            stats,
+            norm_params[max(layer - 1, 0)],
             full_conv[layer],
-            biases[layer + 1],
-            norm_params[layer, 0],
-            norm_params[layer, 1],
-            adjacency,
-            rim_below,
-            rim_above,
-            node_count,
-            dims,
+            biases[layer + 1][None],
+            row_sums,
+            adjacency[:used],
+            10 + (layer > 0) + 2 * used,
         )
-        kept_all.append(kept)
+        xs.append(x)
+        aggs.append(agg)
+        affines.append(affine)
+    totals = group_sum(stats, n_rows) / node_count
+    mean = totals[0]
+    inverse = lax.rsqrt(totals[1] - mean * mean + norm_epsilon)
+    normed = (x - mean) * inverse
+    hidden = norm_params[layers - 1, 0] * normed + norm_params[layers - 1, 1]
+    affines.append(jnp.stack([mean, inverse, mean, inverse]))
     logits = product(hidden, full_head) + head_bias
     log_total = jax.nn.logsumexp(logits, axis=1)
     classes = logits.shape[1]
@@ -367,7 +877,6 @@
     cross = jnp.sum(log_total) - jnp.sum(onehot * logits)
     picks = pair_rows[0, 0]
     sent = logits[picks]
-    block = my_place()[1]
     got = group_gather(sent, n_rows)
     received = got[lax.rem(block + n_rows - jnp.arange(n_rows, dtype=jnp.int32), n_rows)]
     gap = sent - received
@@ -381,23 +890,28 @@
     conv_grads = [None] * layers
     bias_grads = [None] * layers
     norm_grads = [None] * layers
+    stats = jnp.stack([jnp.sum(grad_hidden, 0), jnp.sum(grad_hidden * normed, 0)])
     for layer in reversed(range(layers)):
-        grad_hidden, grad_matrix, grad_bias, grad_gain, grad_shift = layer_backward(
+        norm_grads[layer] = stats[::-1]
+        grad_hidden, conv_grads[layer], grad_bias, stats = backward_layer(
+            n_rows,
+            layer > 0,
+            node_count,
             grad_hidden,
-            kept_all[layer],
-            full_conv[layer],
-            norm_params[layer, 0],
-            adjacency,
-            rim_below,
-            rim_above,
-            node_count,
-            dims,
+            stats,
+            affines[layer + 1],
+            norm_params[layer, 0][None],
+            xs[layer + 1],
+            aggs[layer],
+            xs[layer],
+            affines[layer],
+            w_turned[layer],
+            adjacency[:2],
+            20 + (layer > 0),
         )
-        conv_grads[layer] = grad_matrix
-        bias_grads[layer] = grad_bias
-        norm_grads[layer] = jnp.stack([grad_gain, grad_shift])
+        bias_grads[layer] = grad_bias[0]
     grad_in = product3(inputs.T, grad_hidden)
-    grad_biases = jnp.stack([jnp.sum(grad_hidden, 0)] + bias_grads)
+    grad_biases = jnp.stack([stats[0]] + bias_grads)
     grad_norms = jnp.stack(norm_grads)
     grad_conv = jnp.stack(conv_grads)
     summed = lax.psum(

time: 705 us -> 553 us (0.78)
  Pallas kernels: 84.5 us -> 301 us
  matrix products: 206 us -> 16.2 us
  other arithmetic: 139 us -> 14.2 us
  starting transfers between devices: 33.2 us -> 7.64 us
  local copies, waits for them, and re-layouts: 44.2 us -> 22.7 us
    pallas_call x0 -> x8, Pallas kernels: none -> 269 us  [the longest x3 114 us: forward_layer(): pl.pallas_call(functools.partial(forward_kernel, n, normed, parts, nodes,...]
    dot_general x12 -> x3, matrix products: 107 us -> 5.83 us  [product3(): jnp.matmul(left, right, precision=three_pass, preferred_element_type=f32)]
    unnamed x4 -> x0, other arithmetic: 97.1 us -> none
    dot_general x10 -> x4, matrix products: 97.3 us -> 9.01 us  [product(): jnp.matmul(left, right, precision=highest, preferred_element_type=f32)]
    pallas_call x6 -> x1, Pallas kernels: 58.8 us -> 6.82 us  [group_sum(): pl.pallas_call(functools.partial(group_sum_kernel, n), out_shape=jax.Shap...]
    scatter-add x1 -> x0, local copies, waits for them, and re-layouts: 27.2 us -> none  [per_device(): adjacency = jnp.zeros((rows_dev, rows_dev + 2 * halo_rows), f32).at[edges...]
    ppermute x12 -> x0, starting transfers between devices: 25.6 us -> none  [pass_rows(): lax.ppermute(array, ('batch', 'rows'), flat_pairs(n_batch, n_rows, move))]
    reduce_sum x6 -> x0, other arithmetic: 14 us -> none  [the longest x3 8.34 us: layer_backward(): grad_bias = jnp.sum(grad_pre, 0)]
  transfers between devices with their start and end apart: 21 -> 8, of which waited for: 4 -> 2; matrix products, arithmetic and copies ran while one was open for 36% -> 5% of each run, Pallas kernels for 3% -> 30%
where the time goes in v2:
time: 553 us; the launch traced here: 543 us
  Pallas kernels  301 us (54%)
  waiting for transfers between devices  91.9 us (17%)
  blocking collectives  70.6 us (13%)
  local copies, waits for them, and re-layouts  22.7 us (4%)
  between operations  19.1 us (3%)
  matrix products  16.2 us (3%)
  other arithmetic  14.2 us (3%)
  starting transfers between devices  7.64 us (1%)
    pallas_call x3, Pallas kernels, forward_layer(): pl.pallas_call(functools.partial(forward_kernel, n, normed, parts, nodes,...  114 us
    pallas_call x3, Pallas kernels, backward_layer(): pl.pallas_call(functools.partial(backward_kernel, n, below_normed, nodes,...  112 us
    psum x1, waiting for transfers between devices, per_device(): lax.psum((grad_in, grad_conv, grad_head, grad_biases, grad_norms, grad_he...  72.6 us
    psum x1, blocking collectives, per_device(): lax.psum((grad_in, grad_conv, grad_head, grad_biases, grad_norms, grad_he...  39.3 us
    pallas_call x1, Pallas kernels, fill(): pl.pallas_call(functools.partial(fill_kernel, wide, rim, chunk, parts), o...  35.8 us
    pallas_call x1, Pallas kernels, muon_factors(): pl.pallas_call(functools.partial(muon_kernel, scale_in, scale_head), out_...  18.8 us
    all_gather x1, waiting for transfers between devices, per_device(): lax.all_gather(mom_conv, 'batch', axis=1, tiled=True)  18.6 us
    all_gather x1, blocking collectives, per_device(): lax.all_gather(w_in, 'batch', axis=1, tiled=True)  14.6 us
  transfers between devices with their start and end apart: 8, of which 2 were waited for; matrix products, arithmetic and copies ran while one was open for 5% of the time, Pallas kernels for 30%

profile of v2, /device:TPU:0, one launch (start us, length us, event | category | flops | bytes accessed | tf_op | source)
XLA Modules:
  0.0 543.4 jit_solution(1769265208617246052)
XLA Ops:
  7.2 1.6 collective-permute-start.1
  8.8 1.5 collective-permute-start.2
  10.3 1.8 collective-permute-start
  12.1 1.9 copy.58
  14.0 1.4 collective-permute-start.3
  15.4 1.3 collective-permute-start.4
  16.7 1.3 slice_bitcast_fusion.6
  18.0 1.3 slice_bitcast_fusion.8
  19.3 1.4 fusion.41
  20.8 14.6 %all_gather.18 = f32[100,256]{0,1:T(8,128)S(1)} all-gather(f32[100,64]{0,1:T(8,128)} %param.28), channel_id=1, replica_groups=mesh['batch'=4,'rows'=8] {'batch'}, dimensions={1}, use_global_device_ids=true | all-gather | bytes 128000 | tf_op jit(solution)/shard_map/all_gather | solution.py:826
  35.3 5.5 %all-gather = f32[4,64,47]{1,2,0:T(8,128)S(1)} all-gather(f32[1,64,47]{1,2,0:T(8,128)} %bitcast.84), channel_id=1, replica_groups=mesh['batch'=4,'rows'=8] {'batch'}, dimensions={0}, use_global_device_ids=true | all-gather | bytes 60160 | tf_op jit(solution)/shard_map/all_gather | solution.py:828
  40.9 0.6 pad_clamp_fusion
  42.0 7.1 %order_edges.1 = (s32[128,128]{1,0:T(8,128)S(1)}, f32[128,128]{1,0:T(8,128)S(1)}, bf16[128,128,128]{2,1,0:T(8,128)(2,1)S(1)}, s32[1,128]{1,0:T(1,128)S(1)}, s32[1,128]{1,0:T(1,128)S(1)}) custom-call(s32[128,128]{1,0:T(8,128)S(1)} %bitcast.75, s32[128,128]{1,0:T(8,128)S(1)} %bitcast.74, f32[128,128]{1,0:T(8,128)S(1)} %bitcast.76), custom_call_target="tpu_custom_call" | custom-call | tf_op jit(solution)/shard_map/order_edges/pallas_call | solution.py:300
  49.1 2.0 copy-done.1
  51.1 35.8 %fill_tiles.1 = (bf16[2048,3072]{1,0:T(8,128)(2,1)}, bf16[2048,3072]{1,0:T(8,128)(2,1)}, bf16[2048,3072]{1,0:T(8,128)(2,1)}, f32[2048,128]{1,0:T(8,128)S(1)}) custom-call(s32[1,128]{1,0:T(1,128)S(1)} %get-tuple-element.51.lo, s32[1,128]{1,0:T(1,128)S(1)} %get-tuple-element.52.hi, s32[2]{0:T(128)S(1)} %add_convert_fusion.rims, ...), custom_call_target="tpu_custom_call" | custom-call | tf_op jit(solution)/shard_map/fill_tiles/pallas_call | solution.py:393
  86.9 1.0 copy-done
  87.9 3.3 convolution_add_fusion.x_ref
  91.3 1.5 slice_bitcast_fusion.3
  92.8 1.0 copy.59.w_ref
  93.8 1.0 copy.60.w_ref
  94.8 1.0 copy.61.w_ref
  95.8 0.6 broadcast_in_dim.4.stat_ref
  96.4 40.0 %forward_layer.3 = (f32[2048,256]{1,0:T(8,128)}, f32[2048,256]{1,0:T(8,128)}, f32[2,256]{1,0:T(2,128)}, f32[4,256]{1,0:T(4,128)}) custom-call(f32[2048,256]{1,0:T(8,128)} %convolution_add_fusion.x_ref, f32[2,256]{1,0:T(2,128)} %broadcast_in_dim.4.stat_ref, f32[2,256]{1,0:T(2,128)} %get-tuple-element.172.param_ref, f32[512,256]{1,0:T(8,128)} %copy.59.w_ref, ...), custom_call_target="tpu_custom_call" | custom-call | tf_op jit(solution)/shard_map/forward_layer/pallas_call | solution.py:611
  136.4 36.2 %forward_layer.4 = (f32[2048,256]{1,0:T(8,128)}, f32[2048,256]{1,0:T(8,128)}, f32[2,256]{1,0:T(2,128)}, f32[4,256]{1,0:T(4,128)}) custom-call(f32[2048,256]{1,0:T(8,128)} %get-tuple-element.59.x_ref.act_ref, f32[2,256]{1,0:T(2,128)} %get-tuple-element.60.stat_ref, f32[2,256]{1,0:T(2,128)} %get-tuple-element.172.param_ref, f32[512,256]{1,0:T(8,128)} %copy.60.w_ref, ...), custom_call_target="tpu_custom_call" | custom-call | tf_op jit(solution)/shard_map/forward_layer/pallas_call | solution.py:611
  172.6 37.8 %forward_layer.5 = (f32[2048,256]{1,0:T(8,128)}, f32[2048,256]{1,0:T(8,128)}, f32[2,256]{1,0:T(2,128)}, f32[4,256]{1,0:T(4,128)}) custom-call(f32[2048,256]{1,0:T(8,128)} %get-tuple-element.61.x_ref.act_ref, f32[2,256]{1,0:T(2,128)} %get-tuple-element.62.stat_ref, f32[2,256]{1,0:T(2,128)} %get-tuple-element.171.param_ref, f32[512,256]{1,0:T(8,128)} %copy.61.w_ref, ...), custom_call_target="tpu_custom_call" | custom-call | tf_op jit(solution)/shard_map/forward_layer/pallas_call | solution.py:611
  210.5 6.8 %group_sum.1 = f32[2,256]{1,0:T(2,128)} custom-call(f32[2,256]{1,0:T(2,128)} %get-tuple-element.64.x_ref), custom_call_target="tpu_custom_call" | custom-call | tf_op jit(solution)/shard_map/group_sum/pallas_call | solution.py:119
  217.3 0.7 broadcast_multiply_fusion.2
  218.0 4.0 fusion.43
  222.0 0.6 pad_maximum_fusion.2.affine_ref
  222.6 1.3 copy.64
  223.9 0.7 select_reduce_fusion
  224.6 0.6 fusion.39
  225.3 0.4 copy.65
  225.7 2.4 gather_fusion
  228.1 6.9 %pair_exchange.1 = f32[8,4,47]{2,1,0:T(4,128)} custom-call(f32[8,4,47]{2,1,0:T(4,128)} %bitcast.82), custom_call_target="tpu_custom_call" | custom-call | tf_op jit(solution)/shard_map/pair_exchange/pallas_call | solution.py:156
  235.0 1.4 gather_fusion.1
  236.4 1.3 broadcast_multiply_fusion.1
  237.7 1.1 scatter_fusion
  238.9 3.3 fusion.35
  242.1 1.2 slice_bitcast_fusion
  243.4 0.6 pad_maximum_fusion.4.stat_ref
  244.0 37.7 %backward_layer.3 = (f32[2048,256]{1,0:T(8,128)}, f32[512,256]{1,0:T(8,128)}, f32[1,256]{1,0:T(1,128)}, f32[2,256]{1,0:T(2,128)}) custom-call(f32[2048,256]{1,0:T(8,128)} %get-tuple-element.181.g_ref, f32[2,256]{1,0:T(2,128)} %pad_maximum_fusion.4.stat_ref, f32[4,256]{1,0:T(4,128)} %pad_maximum_fusion.2.affine_ref, f32[1,256]{1,0:T(1,128)} %get-tuple-element.167.gain_ref, ...), custom_call_target="tpu_custom_call" | custom-call | tf_op jit(solution)/shard_map/backward_layer/pallas_call | solution.py:755
  281.7 37.2 %backward_layer.4 = (f32[2048,256]{1,0:T(8,128)}, f32[512,256]{1,0:T(8,128)}, f32[1,256]{1,0:T(1,128)}, f32[2,256]{1,0:T(2,128)}) custom-call(f32[2048,256]{1,0:T(8,128)} %get-tuple-element.67.g_ref, f32[2,256]{1,0:T(2,128)} %get-tuple-element.68.stat_ref, f32[4,256]{1,0:T(4,128)} %get-tuple-element.66.below_ref.affine_ref, ...), custom_call_target="tpu_custom_call" | custom-call | tf_op jit(solution)/shard_map/backward_layer/pallas_call | solution.py:755
  318.9 36.7 %backward_layer.5 = (f32[2048,256]{1,0:T(8,128)}, f32[512,256]{1,0:T(8,128)}, f32[1,256]{1,0:T(1,128)}, f32[2,256]{1,0:T(2,128)}) custom-call(f32[2048,256]{1,0:T(8,128)} %get-tuple-element.71.g_ref, f32[2,256]{1,0:T(2,128)} %get-tuple-element.72.stat_ref, f32[4,256]{1,0:T(4,128)} %get-tuple-element.70.below_ref.affine_ref, ...), custom_call_target="tpu_custom_call" | custom-call | tf_op jit(solution)/shard_map/backward_layer/pallas_call | solution.py:755
  355.6 2.6 pad_maximum_fusion
  358.2 1.5 convolution_bitcast_fusion
  359.9 0.7 all-gather.7.cloned.1.call-update
  360.6 5.4 all_gather.22
  366.1 5.8 %all-gather.1 = f32[4,64,47]{1,2,0:T(8,128)S(1)} all-gather(f32[1,64,47]{1,2,0:T(8,128)S(1)} %bitcast.94), channel_id=1, replica_groups=mesh['batch'=4,'rows'=8] {'batch'}, dimensions={0}, use_global_device_ids=true | all-gather | bytes 60160 | tf_op jit(solution)/shard_map/all_gather | solution.py:831
  375.2 0.3 multiply_reduce_fusion.1
  375.6 1.1 fusion
  376.7 39.3 %all-reduce.2 = (f32[]{:T(128)}, f32[256,47]{0,1:T(8,128)S(1)}, f32[4,256]{1,0:T(4,128)S(1)}, f32[3,2,256]{2,1,0:T(2,128)S(1)}, f32[47]{0:T(128)S(1)}) all-reduce(f32[]{:T(128)S(6)} %add.177, f32[256,47]{0,1:T(8,128)S(1)} %fusion, f32[4,256]{1,0:T(4,128)S(1)} %pad_maximum_fusion.3, ...), channel_id=1, replica_groups=mesh['batch'=4,'rows'=8] {'batch','rows'}, use_global_device_ids=true, to_apply=%region_5.0 | all-reduce | flops 14640 | bytes 117120 | tf_op jit(solution)/shard_map/psum | solution.py:917
  416.7 0.5 multiply_subtract_fusion.2
  417.2 0.6 multiply_subtract_fusion.1
  417.9 0.6 multiply_subtract_fusion
  418.5 72.6 %all-reduce.6.cloned.1.call-done = (f32[100,256]{1,0:T(8,128)}, f32[3,512,256]{2,1,0:T(8,128)}) async-done(((f32[100,256]{1,0:T(8,128)}, f32[3,512,256]{2,1,0:T(8,128)}), (f32[100,256]{1,0:T(8,128)}, f32[3,512,256]{2,1,0:T(8,128)})) %all-reduce.6.cloned.1.call-update) | async-done | bytes 1675280 | tf_op jit(solution)/shard_map/psum | solution.py:917
  491.1 0.9 multiply_add_fusion.4
  492.1 0.7 copy.68
  492.8 18.6 %all-gather.7.cloned.1.call-done = f32[3,512,256]{2,1,0:T(8,128)} async-done(((f32[3,128,256]{2,1,0:T(8,128)}), f32[3,512,256]{2,1,0:T(8,128)}) %all-gather.7.cloned.1.call-update) | async-done | bytes 1572880 | tf_op jit(solution)/shard_map/all_gather | solution.py:830
  511.4 2.1 multiply_add_fusion.3.conv_mom
  513.6 18.8 %muon.1 = (f32[3,256,256]{2,1,0:T(8,128)S(1)}, f32[128,128]{1,0:T(8,128)S(1)}, f32[128,128]{1,0:T(8,128)S(1)}) custom-call(f32[3,512,256]{2,1,0:T(8,128)S(1)} %multiply_add_fusion.3.conv_mom, f32[128,256]{1,0:T(8,128)S(1)} %pad.8.in_mom, f32[128,256]{1,0:T(8,128)S(1)} %pad.9.head_mom), custom_call_target="tpu_custom_call" | custom-call | tf_op jit(solution)/shard_map/muon/pallas_call | solution.py:225
  532.4 0.9 fusion.4
  533.3 0.8 fusion.6
  534.2 1.4 fusion.2
  (113 shorter events, 1.7 us)
Async XLA Ops:
  7.2 84.1 %all-gather.5.cloned.1.call-start = ((), (), s32[]{:S(2)}) async-start(), calls=%async_computation | async-start | bytes 1966080 | tf_op jit(solution)/shard_map/all_gather | solution.py:827
  7.2 34.7 %collective-permute-start.1 = (s32[1,1,2,16384]{3,2,1,0:T(2,128)}, s32[1,1,2,16384]{3,2,1,0:T(2,128)S(1)}, u32[]{:S(2)}, u32[]{:S(2)}) collective-permute-start(s32[1,1,2,16384]{3,2,1,0:T(2,128)} %param.23), channel_id=1, source_target_pairs={{0,0},{1,8},{2,2},{3,10},{4,4},{5,12},{6,6},{7,14},{8,1},{9,9},{10... | collective-permute-start | bytes 393224 | tf_op jit(solution)/shard_map/ppermute | solution.py:58
  8.8 33.2 %collective-permute-start.2 = (f32[1,1,16384]{2,1,0:T(1,128)}, f32[1,1,16384]{2,1,0:T(1,128)S(1)}, u32[]{:S(2)}, u32[]{:S(2)}) collective-permute-start(f32[1,1,16384]{2,1,0:T(1,128)} %param.24), channel_id=1, source_target_pairs={{0,0},{1,8},{2,2},{3,10},{4,4},{5,12},{6,6},{7,14},{8,1},{9,9},{10... | collective-permute-start | bytes 196616 | tf_op jit(solution)/shard_map/ppermute | solution.py:58
  10.3 77.6 %collective-permute-start = (f32[1,2048,100]{1,0,2:T(1,128)}, f32[1,2048,100]{1,0,2:T(1,128)S(1)}, u32[]{:S(2)}, u32[]{:S(2)}) collective-permute-start(f32[1,2048,100]{1,0,2:T(1,128)} %param.22), channel_id=1, source_target_pairs={{0,0},{1,8},{2,2},{3,10},{4,4},{5,12},{6,6},{7,14},{8,1},{9,9},{10... | collective-permute-start | bytes 2457608 | tf_op jit(solution)/shard_map/ppermute | solution.py:58
  14.0 477.1 %all-reduce.6.cloned.1.call-start = ((), (), s32[]{:S(2)}) async-start(), calls=%async_computation.2 | async-start | bytes 3358720 | tf_op jit(solution)/shard_map/psum | solution.py:917
  14.0 209.9 %collective-permute-start.3 = (s32[1,2048]{1,0:T(1,128)}, s32[1,2048]{1,0:T(1,128)S(1)}, u32[]{:S(2)}, u32[]{:S(2)}) collective-permute-start(s32[1,2048]{1,0:T(1,128)} %param.25), channel_id=1, source_target_pairs={{0,0},{1,8},{2,2},{3,10},{4,4},{5,12},{6,6},{7,14},{8,1},{9,9},{10... | collective-permute-start | bytes 24584 | tf_op jit(solution)/shard_map/ppermute | solution.py:58
  15.4 26.3 %collective-permute-start.4 = (s32[1,1,8,4]{2,3,1,0:T(4,128)}, s32[1,1,8,4]{2,3,1,0:T(4,128)S(1)}, u32[]{:S(2)}, u32[]{:S(2)}) collective-permute-start(s32[1,1,8,4]{2,3,1,0:T(4,128)} %param.26), channel_id=1, source_target_pairs={{0,0},{1,8},{2,2},{3,10},{4,4},{5,12},{6,6},{7,14},{8,1},{9,9},{10... | collective-permute-start | bytes 392 | tf_op jit(solution)/shard_map/ppermute | solution.py:58
  19.3 198.6 %copy-start.20 = (f32[1,1,256]{2,1,0:T(1,128)}, f32[1,1,256]{2,1,0:T(1,128)S(1)}, u32[]{:S(2)}) copy-start(f32[1,1,256]{2,1,0:T(1,128)S(1)} %get-tuple-element.169) | copy-start | bytes 3076
  19.3 198.6 %copy-start.22 = (f32[1,1,256]{2,1,0:T(1,128)}, f32[1,1,256]{2,1,0:T(1,128)S(1)}, u32[]{:S(2)}) copy-start(f32[1,1,256]{2,1,0:T(1,128)S(1)} %get-tuple-element.170) | copy-start | bytes 3076
  41.7 176.3 %copy-start.11 = (f32[256,47]{0,1:T(8,128)}, f32[256,47]{0,1:T(8,128)S(1)}, u32[]{:S(2)}) copy-start(f32[256,47]{0,1:T(8,128)S(1)} %reshape.149) | copy-start | bytes 144388
  49.1 2.0 copy-start.1
  86.9 1.0 copy-start
  87.9 4.8 copy-start.5
  172.6 45.4 %copy-start.30 = (f32[47]{0:T(128)S(1)}, f32[47]{0:T(128)}, u32[]{:S(2)}) copy-start(f32[47]{0:T(128)} %param.33) | copy-start | bytes 568
  222.6 16.3 %copy-start.2 = (f32[2048,256]{1,0:T(8,128)S(1)}, f32[2048,256]{1,0:T(8,128)}, u32[]{:S(2)}) copy-start(f32[2048,256]{1,0:T(8,128)} %get-tuple-element.63.act_ref) | copy-start | bytes 6291460
  238.9 3.3 copy-start.4
  318.9 36.7 %copy-start.10 = (f32[512,256]{1,0:T(8,128)S(1)}, f32[512,256]{1,0:T(8,128)}, u32[]{:S(2)}) copy-start(f32[512,256]{1,0:T(8,128)} %get-tuple-element.77) | copy-start | bytes 1572868
  355.6 2.7 copy-start.6
  355.6 2.7 copy-start.7
  358.2 2.3 copy-start.16
  358.2 7.9 %copy-start.17 = (f32[64,47]{0,1:T(8,128)S(1)}, f32[64,47]{0,1:T(8,128)}, u32[]{:S(2)}) copy-start(f32[64,47]{0,1:T(8,128)} %param.36) | copy-start | bytes 36100
  359.7 13.1 %copy-start.25 = (f32[2,256]{1,0:T(2,128)S(1)}, f32[2,256]{1,0:T(2,128)}, u32[]{:S(2)}) copy-start(f32[2,256]{1,0:T(2,128)} %get-tuple-element.72.stat_ref) | copy-start | bytes 6148
  359.7 13.2 %copy-start.24 = (f32[2,256]{1,0:T(2,128)S(1)}, f32[2,256]{1,0:T(2,128)}, u32[]{:S(2)}) copy-start(f32[2,256]{1,0:T(2,128)} %get-tuple-element.68.stat_ref) | copy-start | bytes 6148
  359.7 13.3 %copy-start.18 = (f32[2,256]{1,0:T(2,128)S(1)}, f32[2,256]{1,0:T(2,128)}, u32[]{:S(2)}) copy-start(f32[2,256]{1,0:T(2,128)} %pad_maximum_fusion.4.stat_ref) | copy-start | bytes 6148
  359.7 13.4 %copy-start.37 = (f32[2,256]{1,0:T(2,128)S(1)}, f32[2,256]{1,0:T(2,128)}, u32[]{:S(2)}) copy-start(f32[2,256]{1,0:T(2,128)} %get-tuple-element.82) | copy-start | bytes 6148
  359.7 15.4 %copy-start.32 = (f32[1,256]{1,0:T(1,128)S(1)}, f32[1,256]{1,0:T(1,128)}, u32[]{:S(2)}) copy-start(f32[1,256]{1,0:T(1,128)} %get-tuple-element.85) | copy-start | bytes 3076
  359.7 15.4 %copy-start.33 = (f32[1,256]{1,0:T(1,128)S(1)}, f32[1,256]{1,0:T(1,128)}, u32[]{:S(2)}) copy-start(f32[1,256]{1,0:T(1,128)} %get-tuple-element.84) | copy-start | bytes 3076
  359.7 15.4 %copy-start.34 = (f32[1,256]{1,0:T(1,128)S(1)}, f32[1,256]{1,0:T(1,128)}, u32[]{:S(2)}) copy-start(f32[1,256]{1,0:T(1,128)} %get-tuple-element.83) | copy-start | bytes 3076
  359.8 15.8 %copy-start.3 = (f32[2048,256]{1,0:T(8,128)S(1)}, f32[2048,256]{1,0:T(8,128)}, u32[]{:S(2)}) copy-start(f32[2048,256]{1,0:T(8,128)} %get-tuple-element.63.act_ref) | copy-start | bytes 6291460
  359.8 15.8 %copy-start.21 = (f32[1,1,256]{2,1,0:T(1,128)S(1)}, f32[1,1,256]{2,1,0:T(1,128)}, u32[]{:S(2)}) copy-start(f32[1,1,256]{2,1,0:T(1,128)} %copy-done.20) | copy-start | bytes 3076
  359.8 15.7 %copy-start.23 = (f32[1,1,256]{2,1,0:T(1,128)S(1)}, f32[1,1,256]{2,1,0:T(1,128)}, u32[]{:S(2)}) copy-start(f32[1,1,256]{2,1,0:T(1,128)} %copy-done.22) | copy-start | bytes 3076
  359.8 151.6 %all-gather.7.cloned.1.call-start = ((), (), s32[]{:S(2)}) async-start(), calls=%async_computation.1 | async-start | bytes 1966080 | tf_op jit(solution)/shard_map/all_gather | solution.py:830
  375.2 41.5 %copy-start.31 = (f32[47]{0:T(128)S(1)}, f32[47]{0:T(128)}, u32[]{:S(2)}) copy-start(f32[47]{0:T(128)} %param.33) | copy-start | bytes 568
  375.2 41.5 %copy-start.35 = (f32[47]{0:T(128)S(1)}, f32[47]{0:T(128)}, u32[]{:S(2)}) copy-start(f32[47]{0:T(128)} %param.42) | copy-start | bytes 568
  375.2 41.5 %copy-start.36 = (f32[47]{0:T(128)S(1)}, f32[47]{0:T(128)}, u32[]{:S(2)}) copy-start(f32[47]{0:T(128)} %param.39) | copy-start | bytes 568
  375.2 42.0 %copy-start.19 = (f32[4,256]{1,0:T(4,128)S(1)}, f32[4,256]{1,0:T(4,128)}, u32[]{:S(2)}) copy-start(f32[4,256]{1,0:T(4,128)} %param.31) | copy-start | bytes 12292
  375.2 42.0 %copy-start.28 = (f32[4,256]{1,0:T(4,128)S(1)}, f32[4,256]{1,0:T(4,128)}, u32[]{:S(2)}) copy-start(f32[4,256]{1,0:T(4,128)} %param.40) | copy-start | bytes 12292
  375.2 42.0 %copy-start.29 = (f32[4,256]{1,0:T(4,128)S(1)}, f32[4,256]{1,0:T(4,128)}, u32[]{:S(2)}) copy-start(f32[4,256]{1,0:T(4,128)} %param.37) | copy-start | bytes 12292
  375.5 42.3 %copy-start.15 = (f32[3,2,256]{2,1,0:T(2,128)S(1)}, f32[3,2,256]{2,1,0:T(2,128)}, u32[]{:S(2)}) copy-start(f32[3,2,256]{2,1,0:T(2,128)} %param.32) | copy-start | bytes 18436
  375.5 42.3 %copy-start.26 = (f32[3,2,256]{2,1,0:T(2,128)S(1)}, f32[3,2,256]{2,1,0:T(2,128)}, u32[]{:S(2)}) copy-start(f32[3,2,256]{2,1,0:T(2,128)} %param.41) | copy-start | bytes 18436
  375.6 42.3 %copy-start.27 = (f32[3,2,256]{2,1,0:T(2,128)S(1)}, f32[3,2,256]{2,1,0:T(2,128)}, u32[]{:S(2)}) copy-start(f32[3,2,256]{2,1,0:T(2,128)} %param.38) | copy-start | bytes 18436
  416.7 116.7 %copy-start.13 = (f32[64,47]{0,1:T(8,128)}, f32[64,47]{0,1:T(8,128)S(1)}, u32[]{:S(2)}) copy-start(f32[64,47]{0,1:T(8,128)S(1)} %constant_dynamic-slice_fusion) | copy-start | bytes 36100
  513.5 18.9 %copy-start.12 = (f32[100,64]{0,1:T(8,128)S(1)}, f32[100,64]{0,1:T(8,128)}, u32[]{:S(2)}) copy-start(f32[100,64]{0,1:T(8,128)} %param.28) | copy-start | bytes 76804
  513.5 19.8 %copy-start.14 = (f32[64,47]{0,1:T(8,128)S(1)}, f32[64,47]{0,1:T(8,128)}, u32[]{:S(2)}) copy-start(f32[64,47]{0,1:T(8,128)} %param.30) | copy-start | bytes 36100
  513.5 20.6 %copy-start.8 = (f32[3,128,256]{2,1,0:T(8,128)S(1)}, f32[3,128,256]{2,1,0:T(8,128)}, u32[]{:S(2)}) copy-start(f32[3,128,256]{2,1,0:T(8,128)} %param.29) | copy-start | bytes 1179652
  513.6 21.9 %copy-start.9 = (f32[3,128,256]{2,1,0:T(8,128)}, f32[3,128,256]{2,1,0:T(8,128)S(1)}, u32[]{:S(2)}) copy-start(f32[3,128,256]{2,1,0:T(8,128)S(1)} %constant_dynamic-slice_fusion.1) | copy-start | bytes 1179652
Sparse Core Ops, SparseCore 0:
  14.1 26.2 all-gather.4
  359.9 131.0 all-reduce.5
  492.7 18.6 all-gather.6
